TPU v7x, 256 devices: a whole 4x4x8 slice. The times are simulated.
256 devices in a mesh: head: 4 (over y), seq: 64 (over x, z, core).
Axes of the slice: x: 4, y: 4, z: 8, core: 2. Of those that a mesh axis runs over, the one named last changes fastest.
Arguments:
- queries: bfloat16 [8, 16, 32, 128], P(None, None, 'head'), may hold values from -4000 to 4000
- cache_keys: bfloat16 [16, 16, 8192, 128], P(None, 'head', 'seq'), may hold values from -6 to 6
- stored_values: bfloat16 [16, 16, 8192, 128], P(None, 'head', 'seq'), may hold values from -6 to 6
- new_keys: bfloat16 [8, 16, 16, 128], P(None, None, 'head'), may hold values from -12 to 12
- decoded_values: bfloat16 [8, 16, 16, 128], P(None, None, 'head'), may hold values from -6 to 6
- keep_mask: int32 [16, 8192], P(None, 'seq'), may hold values from 0 to 1
Outputs:
- attended: bfloat16 [8, 16, 4096], P(None, None, 'head')
- importance: float32 [16, 8192], P('head', 'seq')
All inputs are finite; a program needn't handle non-finite values.
Results may differ from a plain program's by a relative error of at most 0.0034.
Values sent between devices are 32-bit elements; how exact they have to be, the bound alone decides.
A program may use at most 128 MiB of HBM per device.

v0:
```python
import jax
import jax.numpy as jnp
from jax import lax
from jax.sharding import Mesh
from jax.sharding import PartitionSpec as P

HQ = 32
BLOCK_TOKENS = 128
DECODE_STEPS = 8
SEQ = ("seq_0", "seq_1", "seq_2")


score_scale = 1.0 / 12.0
far_below = -1e30


def merged_by_axis(x, axes, combine):
    for axis in axes:
        pieces = jax.tree.map(lambda part: lax.all_gather(part, axis), x)
        x = jax.tree.map(lambda part: part[0], pieces)
        for k in range(1, lax.axis_size(axis)):
            x = combine(x, jax.tree.map(lambda part: part[k], pieces))
    return x


def cut_along(x, dim, size):
    shape = x.shape
    blocks = x.reshape(*shape[:dim], size, shape[dim] // size, *shape[dim + 1 :])
    return jnp.moveaxis(blocks, dim, 0)


def sum_at_owner(x, axis, dim):
    blocks = cut_along(x, dim, lax.axis_size(axis))
    arrived = lax.all_to_all(blocks, axis, split_axis=0, concat_axis=0, tiled=True)
    return arrived.sum(axis=0)


def cache_part(grouped_queries, key_cache, value_store_cache, kept):
    count_steps, batch_rows, kv_count, pair_count, head_width = grouped_queries.shape
    block_count = key_cache.shape[2] // BLOCK_TOKENS
    logit_scores = (
        jnp.einsum(
            "tbhgd,bhsd->tbhgs", grouped_queries, key_cache, preferred_element_type=jnp.float32
        )
        * score_scale
    )
    scores_per_block = logit_scores.reshape(
        count_steps, batch_rows, kv_count, pair_count, block_count, BLOCK_TOKENS
    )
    block_keep = kept.reshape(1, batch_rows, 1, 1, block_count, BLOCK_TOKENS)
    block_peak = jnp.max(jnp.where(block_keep, scores_per_block, far_below), axis=-1)
    block_exp = jnp.where(block_keep, jnp.exp(scores_per_block - block_peak[..., None]), 0.0)
    block_total = jnp.sum(block_exp, axis=-1)
    blocked_values = value_store_cache.reshape(
        batch_rows, kv_count, block_count, BLOCK_TOKENS, head_width
    )
    block_sum = jnp.einsum(
        "tbhgks,bhksd->tbhgkd",
        block_exp.astype(jnp.bfloat16),
        blocked_values,
        preferred_element_type=jnp.float32,
    )
    local_peak = jnp.max(block_peak, axis=-1)
    factor = jnp.exp(block_peak - local_peak[..., None])
    local_total = jnp.sum(block_total * factor, axis=-1)
    local_sum = jnp.sum(block_sum * factor[..., None], axis=4)
    return (logit_scores, local_peak, local_total, local_sum)


def combine(earlier, latter):
    peak = jnp.maximum(earlier[0], latter[0])
    first_factor = jnp.exp(earlier[0] - peak)
    second_factor = jnp.exp(latter[0] - peak)
    total = earlier[1] * first_factor + latter[1] * second_factor
    summed = earlier[2] * first_factor[..., None] + latter[2] * second_factor[..., None]
    return (peak, total, summed)


def finish(grouped_queries, totals, logit_scores, kept, fresh_keys, fresh_values, weight):
    count_steps, batch_rows, kv_count, pair_count, head_width = grouped_queries.shape
    cache_peak, cache_total, cache_sum = totals
    new_scores = (
        jnp.einsum(
            "tbhgd,jbhd->tbhgj", grouped_queries, fresh_keys, preferred_element_type=jnp.float32
        )
        * score_scale
    )
    causal = jnp.arange(DECODE_STEPS)[None, :] <= jnp.arange(count_steps)[:, None]
    causal = causal.reshape(count_steps, 1, 1, 1, DECODE_STEPS)
    new_peak = jnp.max(jnp.where(causal, new_scores, far_below), axis=-1)
    new_exp = jnp.where(causal, jnp.exp(new_scores - new_peak[..., None]), 0.0)
    new_total = jnp.sum(new_exp, axis=-1)
    new_sum = jnp.einsum(
        "tbhgj,jbhd->tbhgd",
        new_exp.astype(jnp.bfloat16),
        fresh_values,
        preferred_element_type=jnp.float32,
    )
    peak = jnp.maximum(cache_peak, new_peak)
    cache_factor = jnp.exp(cache_peak - peak)
    new_factor = jnp.exp(new_peak - peak)
    total = cache_total * cache_factor + new_total * new_factor
    weighted = cache_sum * cache_factor[..., None] + new_sum * new_factor[..., None]
    attended = (weighted / total[..., None]).astype(jnp.bfloat16)
    attended = attended.reshape(count_steps, batch_rows, kv_count * pair_count * head_width)
    shares = (
        jnp.where(kept[None, :, None, None, :], jnp.exp(logit_scores - peak[..., None]), 0.0)
        / total[..., None]
    )
    partial_value = jnp.sum(shares, axis=(0, 2, 3)) * weight
    return (attended, partial_value)


def on_device(queries, cache_keys, stored_values, new_keys, decoded_values, keep_mask):
    count_steps, batch_rows, head_count, head_width = queries.shape
    kv_count = cache_keys.shape[1]
    grouped_queries = queries.reshape(
        count_steps, batch_rows, kv_count, head_count // kv_count, head_width
    )
    kept = keep_mask > 0
    weight = keep_mask.shape[1] * lax.axis_size(SEQ) / (DECODE_STEPS * HQ)
    logit_scores, local_peak, local_total, local_sum = cache_part(
        grouped_queries, cache_keys, stored_values, kept
    )
    totals = merged_by_axis((local_peak, local_total, local_sum), SEQ, combine)
    attended, partial_value = finish(
        grouped_queries, totals, logit_scores, kept, new_keys, decoded_values, weight
    )
    importance = sum_at_owner(partial_value, "head", 0)
    return (attended, importance)


def solution(mesh):
    finer = Mesh(
        mesh.devices.reshape(mesh.shape["head"], 4, 8, 2), ("head", "seq_0", "seq_1", "seq_2")
    )
    in_specs = (
        P(None, None, "head", None),
        P(None, "head", SEQ, None),
        P(None, "head", SEQ, None),
        P(None, None, "head", None),
        P(None, None, "head", None),
        P(None, SEQ),
    )
    out_specs = (P(None, None, "head"), P("head", SEQ))
    return jax.shard_map(
        on_device, mesh=finer, in_specs=in_specs, out_specs=out_specs, check_vma=False
    )
```

profile of v0, /device:TPU:1, one launch (start us, length us, event | category | flops | bytes accessed | tf_op | source)
XLA Modules:
  0.0 161.7 jit_solution(13428974618729032064)
XLA Ops:
  7.2 0.8 broadcast_compare_fusion
  8.1 0.7 copy-done
  8.8 2.3 %select_reduce_fusion = (f32[8,16,4,2]{0,3,2,1:T(2,128)S(1)}, f32[8,16,4,2,128]{4,0,3,2,1:T(8,128)S(1)}) fusion(pred[16,128]{1,0:T(8,128)(4,1)S(1)} %broadcast_compare_fusion, bf16[8,16,4,2,128]{4,3,2,1,0:T(2,128)(2,1)} %bitcast.306, bf16[16,4,128,128]{3,2,1,0:T(8,128)(2,1)S(1)} %copy-done), kind=kOutput, calls=%fused_computation.55 | convolution fusion | flops 33946624 | bytes 2889728 | tf_op jit(solution)/shard_map/tbhgd,bhsd->tbhgs/dot_general | solution.py:42
  11.0 0.1 copy.134
  11.1 0.5 fusion.47
  11.7 0.1 copy.136
  11.8 3.1 %fusion.16 = f32[8,16,4,2,1,128]{5,0,3,2,1,4:T(8,128)} fusion(bf16[16,4,128,128]{3,2,1,0:T(8,128)(2,1)} %param.8, f32[8,16,4,2,128]{4,0,3,2,1:T(8,128)S(1)} %get-tuple-element.59, f32[8,16,4,2]{0,3,2,1:T(2,128)S(1)} %copy.136, f32[8,16,4,2]{0,3,2,1:T(2,128)S(1)} %get-tuple-element.58, pred[16,128]{1,0:T(8,128)(4,1)S(1)} %broadcast_compare_fusion), kind=kOutput, calls=%fused_computation.11 | convolution fusion | flops 34078720 | bytes 3155968 | tf_op jit(solution)/shard_map/tbhgks,bhksd->tbhgkd/dot_general | solution.py:57
  15.0 0.1 copy.137
  15.1 10.3 %all-gather.1 = f32[32,16,4,2]{1,2,3,0:T(4,128)S(1)} all-gather(f32[8,16,4,2]{1,2,3,0:T(4,128)S(1)} %copy.137), channel_id=3, replica_groups=mesh['head'=4,'seq_0'=4,'seq_1'=8,'seq_2'=2] {'seq_0'}, dimensions={0}, use_global_device_ids=true | all-gather | bytes 20480 | tf_op jit(solution)/shard_map/all_gather | solution.py:19
  25.5 0.1 copy.141
  25.6 0.1 copy.143
  25.7 0.1 copy.144
  25.8 0.1 copy.146
  25.9 0.1 copy.147
  26.0 0.1 copy.140
  26.2 28.9 %all-gather.11.cloned.1.call-done = f32[32,16,4,2,1,128]{5,0,3,2,1,4:T(8,128)} async-done(((f32[8,16,4,2,1,128]{5,0,3,2,1,4:T(8,128)}), f32[32,16,4,2,1,128]{5,0,3,2,1,4:T(8,128)}) %all-gather.11.cloned.1.call-update) | async-done | bytes 2097168 | tf_op jit(solution)/shard_map/all_gather | solution.py:19
  55.0 2.2 %fusion.34 = f32[1,8,16,4,2,128]{5,1,4,3,2,0:T(8,128)S(1)} fusion(f32[32,16,4,2,1,128]{5,0,3,2,1,4:T(8,128)} %all-gather.11.cloned.1.call-done, f32[8,16,4,2]{0,3,2,1:T(2,128)S(1)} %copy.147, f32[8,16,4,2]{0,3,2,1:T(2,128)S(1)} %copy.146, f32[8,16,4,2]{0,3,2,1:T(2,128)S(1)} %copy.144, f32[8,16,4,2]{0,3,2,1:T(2,128)S(1)} %copy.143, ...), kind=kLoop, calls=%fused_computation.36 | loop fusion | flops 1179648 | bytes 2646016 | tf_op jit(solution)/shard_map/add | solution.py:75
  57.2 1.1 copy.148
  58.4 0.6 copy.175
  59.0 2.2 %fusion.56 = f32[16,4,8,8,2]{3,2,4,1,0:T(8,128)S(1)} fusion(bf16[8,16,4,2,128]{4,3,2,1,0:T(2,128)(2,1)S(1)} %bitcast.307, bf16[8,16,4,128,1]{3,2,1,0,4:T(4,128)(2,1)} %bitcast.308), kind=kOutput, calls=%fused_computation.67 | convolution fusion | flops 2097152 | bytes 425984 | tf_op jit(solution)/shard_map/tbhgd,jbhd->tbhgj/dot_general | solution.py:83
  61.2 0.4 copy.169
  61.6 9.8 %all-gather.2 = f32[32,16,4,2]{1,2,3,0:T(4,128)S(1)} all-gather(f32[8,16,4,2]{1,2,3,0:T(4,128)} %copy.175), channel_id=4, replica_groups=mesh['head'=4,'seq_0'=4,'seq_1'=8,'seq_2'=2] {'seq_0'}, dimensions={0}, use_global_device_ids=true | all-gather | bytes 20480 | tf_op jit(solution)/shard_map/all_gather | solution.py:19
  71.4 23.0 %all_gather.45 = f32[8,8,16,4,2]{2,1,4,3,0:T(8,128)S(1)} all-gather(f32[1,8,16,4,2]{2,1,4,3,0:T(8,128)S(1)} %get-tuple-element.38), channel_id=1, replica_groups=mesh['head'=4,'seq_0'=4,'seq_1'=8,'seq_2'=2] {'seq_1'}, dimensions={0}, use_global_device_ids=true | all-gather | bytes 36864 | tf_op jit(solution)/shard_map/all_gather | solution.py:19
  95.0 22.1 %all_gather.49 = f32[8,8,16,4,2]{2,1,4,3,0:T(8,128)S(1)} all-gather(f32[1,8,16,4,2]{2,1,4,3,0:T(8,128)S(1)} %get-tuple-element.37), channel_id=1, replica_groups=mesh['head'=4,'seq_0'=4,'seq_1'=8,'seq_2'=2] {'seq_1'}, dimensions={0}, use_global_device_ids=true | all-gather | bytes 36864 | tf_op jit(solution)/shard_map/all_gather | solution.py:19
  117.1 0.1 fusion.72
  117.2 12.5 %all_gather.47 = f32[2,8,16,4,2]{2,1,4,3,0:T(8,128)S(1)} all-gather(f32[1,8,16,4,2]{2,1,4,3,0:T(8,128)S(1)} %get-tuple-element.9), channel_id=1, replica_groups=mesh['head'=4,'seq_0'=4,'seq_1'=8,'seq_2'=2] {'seq_2'}, dimensions={0}, use_global_device_ids=true | all-gather | bytes 12288 | tf_op jit(solution)/shard_map/all_gather | solution.py:19
  129.6 1.8 %all_gather.50 = f32[2,8,16,4,2]{2,1,4,3,0:T(8,128)S(1)} all-gather(f32[1,8,16,4,2]{2,1,4,3,0:T(8,128)S(1)} %get-tuple-element.8), channel_id=1, replica_groups=mesh['head'=4,'seq_0'=4,'seq_1'=8,'seq_2'=2] {'seq_2'}, dimensions={0}, use_global_device_ids=true | all-gather | bytes 12288 | tf_op jit(solution)/shard_map/all_gather | solution.py:19
  131.5 5.0 %fusion.20 = f32[1,8,16,4,2,128]{5,2,4,3,1,0:T(8,128)} fusion(f32[8,8,16,4,2,128]{5,2,4,3,1,0:T(8,128)} %all-gather.7.cloned.1.call-done, f32[8,16,4,2]{1,3,2,0:T(2,128)S(1)} %copy.162, f32[8,16,4,2]{1,3,2,0:T(2,128)S(1)} %copy.161, f32[8,16,4,2]{1,3,2,0:T(2,128)S(1)} %copy.160, f32[8,16,4,2]{1,3,2,0:T(2,128)S(1)} %copy.159, f32[8,16,4,2]{1,3,2,0:T(2,128)S(1)} %copy.158, ...), kind=kLoop, calls=%fused_computation.14 | loop fusion | flops 2752512 | bytes 4775936 | tf_op jit(solution)/shard_map/add | solution.py:75
  136.5 0.2 fusion.50
  136.7 0.1 copy.199
  136.8 0.1 copy.200
  136.9 0.1 copy.206
  137.0 0.1 copy.207
  137.1 0.1 copy.192
  137.3 0.2 fusion.59
  137.4 0.1 copy.193
  137.5 0.8 fusion.65
  138.4 0.4 fusion.46
  138.7 0.6 broadcast_multiply_fusion
  139.3 4.1 %all-to-all-start = ((f32[4,4,128]{2,1,0:T(4,128)}), f32[4,4,128]{2,1,0:T(4,128)S(1)}, u32[]{:S(2)}, u32[]{:S(2)}) async-start(f32[4,4,128]{2,1,0:T(4,128)} %bitcast.39), calls=%async_computation | async-start | bytes 16384 | tf_op jit(solution)/shard_map/all_to_all | solution.py:34
  143.4 0.5 copy.172
  143.9 3.7 %all-to-all-done = f32[4,4,128]{2,1,0:T(4,128)S(1)} async-done(((f32[4,4,128]{2,1,0:T(4,128)}), f32[4,4,128]{2,1,0:T(4,128)S(1)}, u32[]{:S(2)}, u32[]{:S(2)}) %all-to-all-start) | async-done | bytes 8224 | tf_op jit(solution)/shard_map/all_to_all | solution.py:34
  147.6 0.6 reduce_sum.50
  148.2 2.6 %all-gather.9.cloned.1.call-done = f32[2,8,16,4,2,128]{5,2,4,3,1,0:T(8,128)} async-done(((f32[1,8,16,4,2,128]{5,2,4,3,1,0:T(8,128)}), f32[2,8,16,4,2,128]{5,2,4,3,1,0:T(8,128)}) %all-gather.9.cloned.1.call-update) | async-done | bytes 1048592 | tf_op jit(solution)/shard_map/all_gather | solution.py:19
  150.8 1.3 fusion.113
  152.1 2.0 %fusion.19 = bf16[8,16,4,2,128]{4,0,3,2,1:T(8,128)(2,1)S(1)} fusion(bf16[8,16,4,2,8]{4,0,3,2,1:T(8,128)(2,1)S(1)} %copy.172, f32[1,8,16,4,2,128]{5,2,4,3,1,0:T(8,128)S(1)} %get-tuple-element.19, f32[1,8,16,4,2,128]{5,2,4,3,1,0:T(8,128)S(1)} %get-tuple-element.18, f32[8,16,4,2]{0,3,2,1:T(2,128)S(1)} %get-tuple-element.2, ...), kind=kOutput, calls=%fused_computation.12 | convolution fusion | flops 3145728 | bytes 1478656 | tf_op jit(solution)/shard_map/tbhgj,jbhd->tbhgd/dot_general | solution.py:93
  154.1 0.2 copy.183
  154.3 0.9 reshape.535
  (40 shorter events, 0.8 us)
Async XLA Ops:
  7.2 1.6 copy-start
  7.2 47.9 %all-gather.11.cloned.1.call-start = ((), (), s32[]{:S(2)}) async-start(), calls=%async_computation.3 | async-start | bytes 2621440 | tf_op jit(solution)/shard_map/all_gather | solution.py:19
  14.9 116.6 %all-gather.7.cloned.1.call-start = ((), (), s32[]{:S(2)}) async-start(), calls=%async_computation.1 | async-start | bytes 4718592 | tf_op jit(solution)/shard_map/all_gather | solution.py:19
  26.1 32.9 %copy-start.1 = (bf16[8,16,8,128]{3,2,1,0:T(8,128)(2,1)S(1)}, bf16[8,16,8,128]{3,2,1,0:T(8,128)(2,1)}, u32[]{:S(2)}) copy-start(bf16[8,16,8,128]{3,2,1,0:T(8,128)(2,1)} %param.6) | copy-start | bytes 786436
  58.4 92.4 %all-gather.9.cloned.1.call-start = ((), (), s32[]{:S(2)}) async-start(), calls=%async_computation.2 | async-start | bytes 1572864 | tf_op jit(solution)/shard_map/all_gather | solution.py:19
  138.4 13.7 %copy-start.2 = (f32[8,16,4,2]{0,3,2,1:T(2,128)S(1)}, f32[8,16,4,2]{0,3,2,1:T(2,128)}, u32[]{:S(2)}) copy-start(f32[8,16,4,2]{0,3,2,1:T(2,128)} %get-tuple-element.6) | copy-start | bytes 12292
  139.3 8.2 %all-to-all-start = ((f32[4,4,128]{2,1,0:T(4,128)}), f32[4,4,128]{2,1,0:T(4,128)S(1)}, u32[]{:S(2)}, u32[]{:S(2)}) async-start(f32[4,4,128]{2,1,0:T(4,128)} %bitcast.39), calls=%async_computation | async-start | bytes 16384 | tf_op jit(solution)/shard_map/all_to_all | solution.py:34
Sparse Core Ops, SparseCore 0:
  15.1 39.9 all-gather.10
  58.5 61.0 all-gather.6
  136.6 14.0 all-gather.8
where the time goes:
time: 162 us
  blocking collectives  79.5 us (49%)
  waiting for transfers between devices  35.2 us (22%)
  between operations  14.1 us (9%)
  other arithmetic  11.5 us (7%)
  matrix products  9.5 us (6%)
  local copies, waits for them, and re-layouts  7.61 us (5%)
  starting transfers between devices  4.2 us (3%)
    all_gather x6, blocking collectives, merged_by_axis(): pieces = jax.tree.map(lambda part: lax.all_gather(part, axis), x)  79.5 us
    all_gather x3, waiting for transfers between devices, merged_by_axis(): pieces = jax.tree.map(lambda part: lax.all_gather(part, axis), x)  31.5 us
    add x2, other arithmetic, combine(): earlier[2] * first_factor[..., None] + latter[2] * second_factor[..., None]  7.13 us
    all_to_all x1, starting transfers between devices, sum_at_owner(): lax.all_to_all(blocks, axis, split_axis=0, concat_axis=0, tiled=True)  4.07 us
    all_to_all x1, waiting for transfers between devices, sum_at_owner(): lax.all_to_all(blocks, axis, split_axis=0, concat_axis=0, tiled=True)  3.66 us
  transfers between devices with their start and end apart: 4, of which 3 were waited for; matrix products, arithmetic and copies ran while one was open for 5% of the time, Pallas kernels for 0%

commit v1 on v0

v1 whole, which is shorter than its diff:
```python
import jax
import jax.numpy as jnp
from jax import lax
from jax.experimental import pallas as pl
from jax.experimental.pallas import tpu as pltpu
from jax.sharding import Mesh
from jax.sharding import PartitionSpec as P

F32 = jnp.float32
BF16 = jnp.bfloat16
MESH = pl.DeviceIdType.MESH
SCALE = 1.0 / 12.0
FAR_BELOW = -1e30

T, B, H, D = 8, 16, 8, 128
KV = 4
S = 128
NY, NX, NZ, NC = 4, 4, 8, 2
FAR_FIRST = (4, 3, 5, 2, 6, 1, 7)
HEADS_ALL = 32
CONTEXT = S * NX * NZ * NC


def lane_of(tile, lane):
    return jnp.broadcast_to(tile[:, lane : lane + 1], (H, D))


def to_front(tile, lane):
    return pltpu.roll(tile, lax.rem(128 - lane, 128), 1)


def expand_heads(rows):
    sub = lax.broadcasted_iota(jnp.int32, (H, D), 0)
    out = jnp.broadcast_to(rows[KV - 1 : KV], (H, D))
    for k in range(KV - 2, -1, -1):
        out = jnp.where(sub < 2 * (k + 1), jnp.broadcast_to(rows[k : k + 1], (H, D)), out)
    return out


def kernel(
    q_hbm, k_hbm, v_hbm, nk_hbm, nv_hbm, mask_hbm,
    out_ref, imp_ref,
    q_ref, k_ref, v_ref, nk_ref, nv_ref, mask_ref,
    sums, exps, peaks, core_in, pair, x_in, x_sum, z_in, gathered, imp_part, imp_in,
    stat_own, stat_core, stat_pair, stat_x, stat_group, stat_z,
    in_sem, kv_sem,
    cs_s, cs_r, cd_s, cd_r, xs_s, xs_r, xd_s, xd_r, zs_s, zs_r, zd_s, zd_r, y_s, y_r,
    gz_s, gz_r, gx_s, gx_r, gc_s, gc_r,
):
    my = lax.axis_index("head")
    mx = lax.axis_index("seq_0")
    mz = lax.axis_index("seq_1")
    mc = lax.axis_index("seq_2")
    other = 1 - mc
    t_own = NX * mc + mx
    b_own = 2 * mz

    def core_dev():
        return {"seq_2": other}

    def x_dev(d):
        return {"seq_0": lax.rem(mx + d, NX)}

    def z_dev(d):
        return {"seq_1": lax.rem(mz + d, NZ)}

    def y_dev(d):
        return {"head": lax.rem(my + d, NY)}

    def remote(src, dst, ss, rs, dev):
        return pltpu.make_async_remote_copy(
            src_ref=src, dst_ref=dst, send_sem=ss, recv_sem=rs, device_id=dev, device_id_type=MESH
        )

    barrier = pltpu.get_barrier_semaphore()
    partners = (
        [core_dev()]
        + [x_dev(d) for d in range(1, NX)]
        + [z_dev(d) for d in FAR_FIRST]
        + [y_dev(d) for d in range(1, NY)]
    )
    for dev in partners:
        pl.semaphore_signal(barrier, inc=1, device_id=dev, device_id_type=MESH)

    small = [
        pltpu.make_async_copy(q_hbm, q_ref, in_sem.at[0]),
        pltpu.make_async_copy(mask_hbm, mask_ref, in_sem.at[1]),
        pltpu.make_async_copy(nk_hbm.at[:, pl.ds(b_own, 2)], nk_ref, in_sem.at[2]),
        pltpu.make_async_copy(nv_hbm.at[:, pl.ds(b_own, 2)], nv_ref, in_sem.at[3]),
    ]
    for copy in small:
        copy.start()

    def k_copy(b):
        return pltpu.make_async_copy(k_hbm.at[b], k_ref.at[b], kv_sem.at[0, b])

    def v_copy(b):
        return pltpu.make_async_copy(v_hbm.at[b], v_ref.at[b], kv_sem.at[1, b])

    def start_loads(b, _):
        k_copy(b).start()
        v_copy(b).start()
        return 0

    lax.fori_loop(0, B, start_loads, 0)
    for copy in small:
        copy.wait()

    lane = lax.broadcasted_iota(jnp.int32, (H, D), 1)
    sub = lax.broadcasted_iota(jnp.int32, (H, D), 0)
    row_kv = lax.rem(lax.broadcasted_iota(jnp.int32, (T * H, S), 0), H) // 2

    def one_row(b, carry):
        peak_tile, total_tile = carry
        k_copy(b).wait()
        v_copy(b).wait()
        q = q_ref[:, b].astype(F32).reshape(T * H, D).astype(BF16)
        scores = lax.dot_general(
            q, k_ref[b].reshape(KV * S, D), (((1,), (1,)), ((), ())), preferred_element_type=F32
        )
        s = scores[:, (KV - 1) * S :]
        for k in range(KV - 2, -1, -1):
            s = jnp.where(row_kv == k, scores[:, k * S : (k + 1) * S], s)
        s = s * SCALE
        keep = jnp.broadcast_to(mask_ref[pl.ds(b, 1), :], (T * H, S)) > 0
        m = jnp.max(jnp.where(keep, s, FAR_BELOW), axis=1, keepdims=True)
        e = jnp.where(keep, jnp.exp(s - m), 0.0)
        total = jnp.sum(e, axis=1, keepdims=True)
        exps[b] = e.reshape(T, H, S)
        weights = jnp.concatenate(
            [jnp.where(row_kv == k, e, 0.0).astype(BF16) for k in range(KV)], axis=1
        )
        o = jnp.dot(weights, v_ref[b].reshape(KV * S, D), preferred_element_type=F32)
        sums[b] = o.reshape(T, H, D)
        for t in range(T):
            here = lane == t * B + b
            peak_tile = jnp.where(here, jnp.broadcast_to(m[t * H : (t + 1) * H], (H, D)), peak_tile)
            total_tile = jnp.where(
                here, jnp.broadcast_to(total[t * H : (t + 1) * H], (H, D)), total_tile
            )
        return peak_tile, total_tile

    zero = jnp.zeros((H, D), F32)
    block_peak, block_total = lax.fori_loop(0, B, one_row, (zero, zero))
    peaks[...] = block_peak

    peak_tile, total_tile = block_peak, block_total
    for i in range(2):
        b = b_own + i
        here = lane == t_own * B + b
        q = q_ref[t_own, b].astype(F32)
        ns = []
        for j in range(T):
            prod = q * expand_heads(nk_ref[j, i].astype(F32))
            sj = jnp.broadcast_to(jnp.sum(prod, axis=1, keepdims=True), (H, D)) * SCALE
            ns.append(jnp.where(j <= t_own, sj, FAR_BELOW))
        new_peak = ns[0]
        for j in range(1, T):
            new_peak = jnp.maximum(new_peak, ns[j])
        new_total, new_sum = zero, zero
        for j in range(T):
            ej = jnp.where(j <= t_own, jnp.exp(ns[j] - new_peak), 0.0)
            new_total = new_total + ej
            new_sum = new_sum + ej.astype(BF16).astype(F32) * expand_heads(nv_ref[j, i].astype(F32))
        old_peak = jnp.max(jnp.where(here, block_peak, -3e38), axis=1, keepdims=True)
        old_total = jnp.sum(jnp.where(here, block_total, 0.0), axis=1, keepdims=True)
        old_peak = jnp.broadcast_to(old_peak, (H, D))
        old_total = jnp.broadcast_to(old_total, (H, D))
        both = jnp.maximum(old_peak, new_peak)
        f_old = jnp.exp(old_peak - both)
        f_new = jnp.exp(new_peak - both)
        sums[b, t_own] = sums[b, t_own] * f_old + new_sum * f_new
        peak_tile = jnp.where(here, both, peak_tile)
        total_tile = jnp.where(here, old_total * f_old + new_total * f_new, total_tile)
    stat_own[0] = peak_tile
    stat_own[1] = total_tile

    pl.semaphore_wait(barrier, len(partners))

    order = [lax.rem(mz + d, NZ) for d in FAR_FIRST] + [mz]
    core_stat = remote(stat_own, stat_core, cs_s, cs_r, core_dev())
    core_stat.start()
    core_copies = []
    for k, zz in enumerate(order):
        copy = remote(
            sums.at[pl.ds(2 * zz, 2), pl.ds(NX * other, NX)],
            core_in.at[k],
            cd_s.at[k],
            cd_r.at[k],
            core_dev(),
        )
        copy.start()
        core_copies.append(copy)
    core_stat.wait_recv()
    peak_c, total_c = stat_core[0], stat_core[1]
    pair_peak = jnp.maximum(peak_tile, peak_c)
    f_own = jnp.exp(peak_tile - pair_peak)
    f_core = jnp.exp(peak_c - pair_peak)
    pair_total = total_tile * f_own + total_c * f_core
    stat_pair[0] = pair_peak
    stat_pair[1] = pair_total

    x_stats = []
    for d in range(1, NX):
        copy = remote(stat_pair, stat_x.at[d - 1], xs_s.at[d - 1], xs_r.at[d - 1], x_dev(d))
        copy.start()
        x_stats.append(copy)
    x_copies = []
    for k, zz in enumerate(order):
        core_copies[k].wait_recv()
        fo = to_front(f_own, NX * mc * B + 2 * zz)
        fc = to_front(f_core, NX * mc * B + 2 * zz)
        for tl in range(NX):
            for i in range(2):
                at = tl * B + i
                pair[k, tl, i] = (
                    sums[2 * zz + i, NX * mc + tl] * lane_of(fo, at)
                    + core_in[k, i, tl] * lane_of(fc, at)
                )
        row = []
        for d in (2, 1, 3):
            copy = remote(
                pair.at[k, lax.rem(mx + d, NX)],
                x_in.at[k, d - 1],
                xd_s.at[k, d - 1],
                xd_r.at[k, d - 1],
                x_dev(d),
            )
            copy.start()
            row.append(copy)
        x_copies.append(row)
    for copy in x_stats:
        copy.wait_recv()
    group_peak = pair_peak
    for d in range(1, NX):
        group_peak = jnp.maximum(group_peak, stat_x[d - 1, 0])
    f_mine = jnp.exp(pair_peak - group_peak)
    group_total = pair_total * f_mine
    f_peer = []
    for d in range(1, NX):
        f = jnp.exp(stat_x[d - 1, 0] - group_peak)
        f_peer.append(f)
        group_total = group_total + stat_x[d - 1, 1] * f
    stat_group[0] = group_peak
    stat_group[1] = group_total

    z_stats = []
    for d in FAR_FIRST:
        copy = remote(stat_group, stat_z.at[d - 1], zs_s.at[d - 1], zs_r.at[d - 1], z_dev(d))
        copy.start()
        z_stats.append(copy)
    z_copies = []
    for k, zz in enumerate(order):
        for copy in x_copies[k]:
            copy.wait_recv()
        front = t_own * B + 2 * zz
        fm = to_front(f_mine, front)
        fp = [to_front(f, front) for f in f_peer]
        for i in range(2):
            acc = pair[k, mx, i] * lane_of(fm, i)
            for d in range(1, NX):
                acc = acc + x_in[k, d - 1, i] * lane_of(fp[d - 1], i)
            x_sum[k, i] = acc
        if k < NZ - 1:
            d = FAR_FIRST[k]
            copy = remote(x_sum.at[k], z_in.at[d - 1], zd_s.at[d - 1], zd_r.at[d - 1], z_dev(d))
            copy.start()
            z_copies.append(copy)
    for copy in z_stats:
        copy.wait_recv()
    peak = group_peak
    for d in range(1, NZ):
        peak = jnp.maximum(peak, stat_z[d - 1, 0])
    f_mine = jnp.exp(group_peak - peak)
    total = group_total * f_mine
    f_peer = []
    for d in range(1, NZ):
        f = jnp.exp(stat_z[d - 1, 0] - peak)
        f_peer.append(f)
        total = total + stat_z[d - 1, 1] * f
    inverse = 1.0 / total
    front = t_own * B + b_own
    fm = to_front(f_mine * inverse, front)
    fp = [to_front(f * inverse, front) for f in f_peer]
    for copy in z_copies:
        copy.wait_recv()
    for i in range(2):
        acc = x_sum[NZ - 1, i] * lane_of(fm, i)
        for d in range(1, NZ):
            acc = acc + z_in[d - 1, i] * lane_of(fp[d - 1], i)
        gathered[t_own, b_own + i] = acc

    def piece(t, zz):
        return gathered.at[t, pl.ds(2 * zz, 2)]

    gz = {}
    for d in FAR_FIRST:
        copy = remote(piece(t_own, mz), piece(t_own, mz), gz_s.at[d - 1], gz_r.at[d - 1], z_dev(d))
        copy.start()
        gz[d] = copy
    gx, gc = {}, {}

    def forward_x(d):
        zz = lax.rem(mz + NZ - d, NZ)
        for dx in (2, 1, 3):
            copy = remote(
                piece(t_own, zz), piece(t_own, zz), gx_s.at[d, dx - 1], gx_r.at[d, dx - 1], x_dev(dx)
            )
            copy.start()
            gx[d, dx] = copy

    def forward_core(d, dx):
        zz = lax.rem(mz + NZ - d, NZ)
        t = NX * mc + lax.rem(mx + NX - dx, NX)
        copy = remote(piece(t, zz), piece(t, zz), gc_s.at[d, dx], gc_r.at[d, dx], core_dev())
        copy.start()
        gc[d, dx] = copy

    forward_x(0)
    forward_core(0, 0)

    share = jnp.exp(peaks[...] - peak) * inverse * (CONTEXT / (DECODE * HEADS_ALL))
    for b in range(B):
        acc = exps[b, 0] * lane_of(share, b)
        for t in range(1, T):
            acc = acc + exps[b, t] * lane_of(share, t * B + b)
        imp_part[b // 4, pl.ds(b % 4, 1)] = jnp.sum(acc, axis=0, keepdims=True)
    y_copies = []
    for d in range(1, NY):
        copy = remote(
            imp_part.at[lax.rem(my + d, NY)], imp_in.at[d - 1], y_s.at[d - 1], y_r.at[d - 1], y_dev(d)
        )
        copy.start()
        y_copies.append(copy)

    def take_z(d):
        gz[d].wait_recv()
        forward_x(d)
        forward_core(d, 0)

    def take_x(d, dx):
        gx[d, dx].wait_recv()
        forward_core(d, dx)

    take_z(1)
    take_z(7)
    take_x(0, 1)
    take_x(0, 3)
    take_z(2)
    take_z(6)
    take_x(0, 2)
    take_z(3)
    take_z(5)
    take_z(4)
    for copy in y_copies:
        copy.wait_recv()
    imp_ref[...] = imp_part[my] + imp_in[0] + imp_in[1] + imp_in[2]
    for d in (1, 7, 2, 6, 3, 5, 4):
        for dx in (1, 3, 2):
            take_x(d, dx)
    for d in (0, 1, 7, 2, 6, 3, 5, 4):
        for dx in (0, 1, 3, 2):
            gc[d, dx].wait_recv()

    for t in range(T):
        for h in range(H):
            out_ref[t, :, h * D : (h + 1) * D] = gathered[t, :, h, :].astype(BF16)

    for copy in (
        [core_stat] + core_copies + x_stats + [c for r in x_copies for c in r]
        + z_stats + z_copies + y_copies + list(gz.values()) + list(gx.values()) + list(gc.values())
    ):
        copy.wait_send()


DECODE = T


def on_device(queries, cache_keys, stored_values, new_keys, decoded_values, keep_mask):
    any_space = pl.BlockSpec(memory_space=pltpu.MemorySpace.HBM)
    vmem = pl.BlockSpec(memory_space=pltpu.VMEM)
    dma = pltpu.SemaphoreType.DMA
    return pl.pallas_call(
        kernel,
        out_shape=(
            jax.ShapeDtypeStruct((T, B, H * D), BF16),
            jax.ShapeDtypeStruct((B // NY, S), F32),
        ),
        in_specs=[any_space] * 6,
        out_specs=(vmem, vmem),
        scratch_shapes=[
            pltpu.VMEM((T, B, H, D), BF16),
            pltpu.VMEM((B, KV, S, D), BF16),
            pltpu.VMEM((B, KV, S, D), BF16),
            pltpu.VMEM((T, 2, KV, D), BF16),
            pltpu.VMEM((T, 2, KV, D), BF16),
            pltpu.VMEM((B, S), jnp.int32),
            pltpu.VMEM((B, T, H, D), F32),
            pltpu.VMEM((B, T, H, S), F32),
            pltpu.VMEM((H, D), F32),
            pltpu.VMEM((NZ, 2, NX, H, D), F32),
            pltpu.VMEM((NZ, NX, 2, H, D), F32),
            pltpu.VMEM((NZ, NX - 1, 2, H, D), F32),
            pltpu.VMEM((NZ, 2, H, D), F32),
            pltpu.VMEM((NZ - 1, 2, H, D), F32),
            pltpu.VMEM((T, B, H, D), F32),
            pltpu.VMEM((NY, B // NY, S), F32),
            pltpu.VMEM((NY - 1, B // NY, S), F32),
            pltpu.VMEM((2, H, D), F32),
            pltpu.VMEM((2, H, D), F32),
            pltpu.VMEM((2, H, D), F32),
            pltpu.VMEM((NX - 1, 2, H, D), F32),
            pltpu.VMEM((2, H, D), F32),
            pltpu.VMEM((NZ - 1, 2, H, D), F32),
            dma((4,)),
            dma((2, B)),
            dma, dma, dma((NZ,)), dma((NZ,)),
            dma((NX - 1,)), dma((NX - 1,)), dma((NZ, NX - 1)), dma((NZ, NX - 1)),
            dma((NZ - 1,)), dma((NZ - 1,)), dma((NZ - 1,)), dma((NZ - 1,)),
            dma((NY - 1,)), dma((NY - 1,)),
            dma((NZ - 1,)), dma((NZ - 1,)), dma((NZ, NX - 1)), dma((NZ, NX - 1)),
            dma((NZ, NX)), dma((NZ, NX)),
        ],
        compiler_params=pltpu.CompilerParams(
            collective_id=0, has_side_effects=True, vmem_limit_bytes=63 << 20
        ),
    )(queries, cache_keys, stored_values, new_keys, decoded_values, keep_mask)


def solution(mesh):
    finer = Mesh(
        mesh.devices.reshape(mesh.shape["head"], NX, NZ, NC), ("head", "seq_0", "seq_1", "seq_2")
    )
    seq = ("seq_0", "seq_1", "seq_2")
    in_specs = (
        P(None, None, "head", None),
        P(None, "head", seq, None),
        P(None, "head", seq, None),
        P(None, None, "head", None),
        P(None, None, "head", None),
        P(None, seq),
    )
    out_specs = (P(None, None, "head"), P("head", seq))
    return jax.shard_map(
        on_device, mesh=finer, in_specs=in_specs, out_specs=out_specs, check_vma=False
    )
```

time: 162 us -> 40.5 us (0.25)
  blocking collectives: 79.5 us -> 0 us
  Pallas kernels: 0 us -> 36.8 us
  waiting for transfers between devices: 35.2 us -> 0 us
  between operations: 14.1 us -> 0.64 us
  other arithmetic: 11.5 us -> 0 us
  matrix products: 9.5 us -> 0 us
  local copies, waits for them, and re-layouts: 7.61 us -> 2.92 us
  starting transfers between devices: 4.2 us -> 0 us
    all_gather x6 -> x0, blocking collectives: 79.5 us -> none  [merged_by_axis(): pieces = jax.tree.map(lambda part: lax.all_gather(part, axis), x)]
    pallas_call x0 -> x1, Pallas kernels: none -> 36.8 us  [on_device(): pl.pallas_call(kernel, out_shape=(jax.ShapeDtypeStruct((T, B, H * D), BF1...]
    all_gather x3 -> x0, waiting for transfers between devices: 31.5 us -> none  [merged_by_axis(): pieces = jax.tree.map(lambda part: lax.all_gather(part, axis), x)]
    dot_general x4 -> x0, matrix products: 9.5 us -> none  [the longest x1 3.11 us: cache_part(): jnp.einsum('tbhgks,bhksd->tbhgkd', block_exp.astype(jnp.bfloat16), blocke...]
    add x5 -> x0, other arithmetic: 8.1 us -> none  [the longest x2 7.13 us: combine(): earlier[2] * first_factor[..., None] + latter[2] * second_factor[..., None]]
    all_to_all x1 -> x0, starting transfers between devices: 4.07 us -> none  [sum_at_owner(): lax.all_to_all(blocks, axis, split_axis=0, concat_axis=0, tiled=True)]
    all_to_all x1 -> x0, waiting for transfers between devices: 3.66 us -> none  [sum_at_owner(): lax.all_to_all(blocks, axis, split_axis=0, concat_axis=0, tiled=True)]
  transfers between devices with their start and end apart: 4 -> 0, of which waited for: 3 -> 0; matrix products, arithmetic and copies ran while one was open for 5% -> 0% of each run, Pallas kernels for 0% -> 0%
where the time goes in v1:
time: 40.5 us; the launch traced here: 40.4 us
  Pallas kernels  36.8 us (91%)
  local copies, waits for them, and re-layouts  2.92 us (7%)
  between operations  0.64 us (2%)
    pallas_call x1, Pallas kernels, on_device(): pl.pallas_call(kernel, out_shape=(jax.ShapeDtypeStruct((T, B, H * D), BF1...  36.8 us
    unnamed x2, local copies, waits for them, and re-layouts  2.92 us

profile of v1, /device:TPU:1, one launch (start us, length us, event | category | flops | bytes accessed | tf_op | source)
XLA Modules:
  0.0 40.4 jit_solution(3807731190318620476)
XLA Ops:
  0.6 36.8 %shard_map.77 = (bf16[8,16,1024]{2,1,0:T(8,128)(2,1)}, f32[4,128]{1,0:T(4,128)}) custom-call(bf16[8,16,8,128]{3,2,1,0:T(8,128)(2,1)} %q_hbm.1, bf16[16,4,128,128]{3,2,1,0:T(8,128)(2,1)} %k_hbm.1, bf16[16,4,128,128]{3,2,1,0:T(8,128)(2,1)} %v_hbm.1, bf16[8,16,4,128]{3,2,1,0:T(4,128)(2,1)} %nk_hbm.1, bf16[8,16,4,128]{3,2,1,0:T(4,128)(2,1)} %nv_hbm.1, ...), custom_call_target="tpu_custom_call" | custom-call | tf_op jit(solution)/shard_map/pallas_call | solution.py:383
  37.4 1.7 %copy.10 = bf16[8,16,1024]{2,1,0:T(8,128)(2,1)} copy(bf16[8,16,1024]{2,1,0:T(8,128)(2,1)} %get-tuple-element.4) | data formatting | bytes 524288
  39.1 1.2 %copy.11 = f32[4,128]{1,0:T(4,128)} copy(f32[4,128]{1,0:T(4,128)} %get-tuple-element.5) | data formatting | bytes 4096

commit v2 on v1

v2 whole, which is shorter than its diff:
```python
import jax
import jax.numpy as jnp
from jax import lax
from jax.experimental import pallas as pl
from jax.experimental.pallas import tpu as pltpu
from jax.sharding import Mesh
from jax.sharding import PartitionSpec as P

F32 = jnp.float32
BF16 = jnp.bfloat16
MESH = pl.DeviceIdType.MESH
SCALE = 1.0 / 12.0
FAR_BELOW = -1e30

T, B, H, D = 8, 16, 8, 128
KV = 4
S = 128
NY, NX, NZ, NC = 4, 4, 8, 2
FAR_FIRST = (4, 3, 5, 2, 6, 1, 7)
SLOT = [(d + 2) % NZ for d in range(NZ)]
FAR, NEAR = (5, 3), (0, 5)
HEADS_ALL = 32
CONTEXT = S * NX * NZ * NC


def lane_of(tile, lane):
    return jnp.broadcast_to(tile[:, lane : lane + 1], (H, D))


def to_front(tile, lane):
    return pltpu.roll(tile, lax.rem(128 - lane, 128), 1)


def expand_heads(rows):
    sub = lax.broadcasted_iota(jnp.int32, (H, D), 0)
    out = jnp.broadcast_to(rows[KV - 1 : KV], (H, D))
    for k in range(KV - 2, -1, -1):
        out = jnp.where(sub < 2 * (k + 1), jnp.broadcast_to(rows[k : k + 1], (H, D)), out)
    return out


def kernel(
    q_hbm, k_hbm, v_hbm, nk_hbm, nv_hbm, mask_hbm,
    out_ref, imp_ref,
    q_ref, k_ref, v_ref, nk_ref, nv_ref, mask_ref,
    sums, exps, peaks, core_in, pair, x_in, z_out, z_in, gathered, imp_part, imp_in,
    f_pair, f_x, stat_own, stat_core, stat_pair, stat_x, stat_group, stat_z,
    in_sem, chunk_sem,
    cs_s, cs_r, cd_s, cd_r, xs_s, xs_r, xd_s, xd_r, zs_s, zs_r, zd_s, zd_r, y_s, y_r,
    gz_s, gz_r, gx_s, gx_r, gc_s, gc_r,
):
    my = lax.axis_index("head")
    mx = lax.axis_index("seq_0")
    mz = lax.axis_index("seq_1")
    mc = lax.axis_index("seq_2")
    other = 1 - mc
    t_half = NX * mc
    t_own = t_half + mx
    base = lax.rem(mz + NZ - 2, NZ)

    def core_dev():
        return {"seq_2": other}

    def x_dev(d):
        return {"seq_0": lax.rem(mx + d, NX)}

    def z_dev(d):
        return {"seq_1": lax.rem(mz + d, NZ)}

    def y_dev(d):
        return {"head": lax.rem(my + d, NY)}

    started = []

    def remote(src, dst, ss, rs, dev):
        copy = pltpu.make_async_remote_copy(
            src_ref=src, dst_ref=dst, send_sem=ss, recv_sem=rs, device_id=dev, device_id_type=MESH
        )
        copy.start()
        started.append(copy)
        return copy

    barrier = pltpu.get_barrier_semaphore()
    partners = (
        [z_dev(d) for d in FAR_FIRST]
        + [x_dev(d) for d in (2, 1, 3)]
        + [y_dev(d) for d in (2, 1, 3)]
        + [core_dev()]
    )
    for dev in partners:
        pl.semaphore_signal(barrier, inc=1, device_id=dev, device_id_type=MESH)

    def chunk_loads(slot):
        rows = pl.ds(2 * lax.rem(base + slot, NZ), 2)
        mine = pl.ds(2 * slot, 2)
        return [
            pltpu.make_async_copy(q_hbm.at[:, rows], q_ref.at[:, mine], chunk_sem.at[0, slot]),
            pltpu.make_async_copy(k_hbm.at[rows], k_ref.at[mine], chunk_sem.at[1, slot]),
            pltpu.make_async_copy(v_hbm.at[rows], v_ref.at[mine], chunk_sem.at[2, slot]),
        ]

    b_own = 2 * mz
    small = [
        pltpu.make_async_copy(mask_hbm, mask_ref, in_sem.at[0]),
        pltpu.make_async_copy(nk_hbm.at[:, pl.ds(b_own, 2)], nk_ref, in_sem.at[1]),
        pltpu.make_async_copy(nv_hbm.at[:, pl.ds(b_own, 2)], nv_ref, in_sem.at[2]),
    ]
    small[0].start()
    loads = {slot: chunk_loads(slot) for slot in range(NZ)}
    batches = ((4, 5, 6, 7), (0, 1, 2, 3))
    for slots in batches:
        for slot in slots:
            for copy in loads[slot]:
                copy.start()
    for copy in small[1:]:
        copy.start()
    small[0].wait()

    lane = lax.broadcasted_iota(jnp.int32, (H, D), 1)
    row_kv = lax.rem(lax.broadcasted_iota(jnp.int32, (T * H, S), 0), H) // 2

    zero = jnp.zeros((H, D), F32)
    block_peak, block_total = zero, zero
    for slots in batches:
        for slot in slots:
            for copy in loads[slot]:
                copy.wait()
        rows = [2 * slot + i for slot in slots for i in range(2)]
        scores = []
        for r in rows:
            q = q_ref[:, r].astype(F32).reshape(T * H, D).astype(BF16)
            wide = lax.dot_general(
                q, k_ref[r].reshape(KV * S, D), (((1,), (1,)), ((), ())), preferred_element_type=F32
            )
            s = wide[:, (KV - 1) * S :]
            for k in range(KV - 2, -1, -1):
                s = jnp.where(row_kv == k, wide[:, k * S : (k + 1) * S], s)
            scores.append(s * SCALE)
        weights = []
        for r, s in zip(rows, scores):
            b = lax.rem(2 * base + r, B)
            keep = jnp.broadcast_to(mask_ref[pl.ds(b, 1), :], (T * H, S)) > 0
            m = jnp.max(jnp.where(keep, s, FAR_BELOW), axis=1, keepdims=True)
            e = jnp.where(keep, jnp.exp(s - m), 0.0)
            total = jnp.sum(e, axis=1, keepdims=True)
            exps[r] = e.reshape(T, H, S)
            weights.append(e)
            for t in range(T):
                here = lane == t * B + r
                part = slice(t * H, (t + 1) * H)
                block_peak = jnp.where(here, jnp.broadcast_to(m[part], (H, D)), block_peak)
                block_total = jnp.where(here, jnp.broadcast_to(total[part], (H, D)), block_total)
        for r, e in zip(rows, weights):
            wide = jnp.concatenate(
                [jnp.where(row_kv == k, e, 0.0).astype(BF16) for k in range(KV)], axis=1
            )
            o = jnp.dot(wide, v_ref[r].reshape(KV * S, D), preferred_element_type=F32)
            sums[r] = o.reshape(T, H, D)
    peaks[...] = block_peak

    peak_tile, total_tile = block_peak, block_total
    for copy in small[1:]:
        copy.wait()
    for i in range(2):
        r = 2 * SLOT[0] + i
        here = lane == t_own * B + r
        q = q_ref[t_own, r].astype(F32)
        ns = []
        for j in range(T):
            prod = q * expand_heads(nk_ref[j, i].astype(F32))
            sj = jnp.broadcast_to(jnp.sum(prod, axis=1, keepdims=True), (H, D)) * SCALE
            ns.append(jnp.where(j <= t_own, sj, FAR_BELOW))
        new_peak = ns[0]
        for j in range(1, T):
            new_peak = jnp.maximum(new_peak, ns[j])
        new_total, new_sum = zero, zero
        for j in range(T):
            ej = jnp.where(j <= t_own, jnp.exp(ns[j] - new_peak), 0.0)
            new_total = new_total + ej
            new_sum = new_sum + ej.astype(BF16).astype(F32) * expand_heads(nv_ref[j, i].astype(F32))
        old_peak = jnp.max(jnp.where(here, block_peak, -3e38), axis=1, keepdims=True)
        old_total = jnp.sum(jnp.where(here, block_total, 0.0), axis=1, keepdims=True)
        old_peak = jnp.broadcast_to(old_peak, (H, D))
        old_total = jnp.broadcast_to(old_total, (H, D))
        both = jnp.maximum(old_peak, new_peak)
        f_old = jnp.exp(old_peak - both)
        f_new = jnp.exp(new_peak - both)
        sums[r, t_own] = sums[r, t_own] * f_old + new_sum * f_new
        peak_tile = jnp.where(here, both, peak_tile)
        total_tile = jnp.where(here, old_total * f_old + new_total * f_new, total_tile)
    stat_own[0] = peak_tile
    stat_own[1] = total_tile

    pl.semaphore_wait(barrier, len(partners))

    core_stat = remote(stat_own, stat_core, cs_s, cs_r, core_dev())
    core_copies = []
    for g, (first, count) in enumerate((FAR, NEAR)):
        rows = pl.ds(2 * first, 2 * count)
        core_copies.append(
            remote(
                sums.at[rows, pl.ds(NX * other, NX)], core_in.at[rows], cd_s.at[g], cd_r.at[g],
                core_dev(),
            )
        )
    core_stat.wait_recv()
    peak_c, total_c = stat_core[0], stat_core[1]
    pair_peak = jnp.maximum(peak_tile, peak_c)
    f_own = jnp.exp(peak_tile - pair_peak)
    f_core = jnp.exp(peak_c - pair_peak)
    pair_total = total_tile * f_own + total_c * f_core
    stat_pair[0] = pair_peak
    stat_pair[1] = pair_total

    x_stats = []
    for d in (2, 1, 3):
        x_stats.append(
            remote(stat_pair, stat_x.at[d - 1], xs_s.at[d - 1], xs_r.at[d - 1], x_dev(d))
        )
    fo = to_front(f_own, t_half * B)
    fc = to_front(f_core, t_half * B)
    for first, count in (FAR, NEAR):
        for tl in range(NX):
            for r in range(2 * first, 2 * (first + count)):
                f_pair[0, tl, r] = lane_of(fo, tl * B + r)
                f_pair[1, tl, r] = lane_of(fc, tl * B + r)
    x_copies = []
    for g, (first, count) in enumerate((FAR, NEAR)):
        core_copies[g].wait_recv()
        for tl in range(NX):
            for r in range(2 * first, 2 * (first + count)):
                pair[tl, r] = (
                    sums[r, t_half + tl] * f_pair[0, tl, r] + core_in[r, tl] * f_pair[1, tl, r]
                )
        rows = pl.ds(2 * first, 2 * count)
        x_copies.append(
            [
                remote(
                    pair.at[lax.rem(mx + d, NX), rows], x_in.at[d - 1, rows],
                    xd_s.at[g, d - 1], xd_r.at[g, d - 1], x_dev(d),
                )
                for d in (2, 1, 3)
            ]
        )
    for copy in x_stats:
        copy.wait_recv()
    group_peak = pair_peak
    for d in range(1, NX):
        group_peak = jnp.maximum(group_peak, stat_x[d - 1, 0])
    factors = [jnp.exp(pair_peak - group_peak)]
    group_total = pair_total * factors[0]
    for d in range(1, NX):
        f = jnp.exp(stat_x[d - 1, 0] - group_peak)
        factors.append(f)
        group_total = group_total + stat_x[d - 1, 1] * f

    shift = 2 * base
    in_row = lax.rem(lane, B)

    def by_row(tile):
        return jnp.where(
            in_row >= shift, pltpu.roll(tile, shift, 1), pltpu.roll(tile, lax.rem(shift + 112, 128), 1)
        )

    def by_slot(tile):
        return jnp.where(
            in_row < B - shift,
            pltpu.roll(tile, lax.rem(128 - shift, 128), 1),
            pltpu.roll(tile, lax.rem(144 - shift, 128), 1),
        )

    group_peak = by_row(group_peak)
    group_total = by_row(group_total)
    stat_group[0] = group_peak
    stat_group[1] = group_total
    z_stats = [
        remote(stat_group, stat_z.at[d - 1], zs_s.at[d - 1], zs_r.at[d - 1], z_dev(d))
        for d in FAR_FIRST
    ]
    for d in range(NX):
        f = to_front(factors[d], t_own * B)
        for r in range(B):
            f_x[d, r] = lane_of(f, r)
    z_copies = []
    for g, sends in enumerate(((4, 3, 5), (2, 6, 1, 7, 0))):
        for copy in x_copies[g]:
            copy.wait_recv()
        for d in sends:
            for i in range(2):
                r = 2 * SLOT[d] + i
                acc = pair[mx, r] * f_x[0, r]
                for dx in range(1, NX):
                    acc = acc + x_in[dx - 1, r] * f_x[dx, r]
                z_out[SLOT[d], i] = acc
            if d > 0:
                z_copies.append(
                    remote(
                        z_out.at[SLOT[d]], z_in.at[d - 1], zd_s.at[d - 1], zd_r.at[d - 1], z_dev(d)
                    )
                )
    for copy in z_stats:
        copy.wait_recv()
    peak = group_peak
    for d in range(1, NZ):
        peak = jnp.maximum(peak, stat_z[d - 1, 0])
    factors = [jnp.exp(group_peak - peak)]
    total = group_total * factors[0]
    for d in range(1, NZ):
        f = jnp.exp(stat_z[d - 1, 0] - peak)
        factors.append(f)
        total = total + stat_z[d - 1, 1] * f
    inverse = 1.0 / total
    front = [to_front(f * inverse, t_own * B + b_own) for f in factors]
    scale = [[lane_of(f, i) for f in front] for i in range(2)]
    share = jnp.exp(peaks[...] - by_slot(peak)) * by_slot(inverse) * (CONTEXT / (T * HEADS_ALL))
    for copy in z_copies:
        copy.wait_recv()
    for i in range(2):
        acc = z_out[SLOT[0], i] * scale[i][0]
        for d in range(1, NZ):
            acc = acc + z_in[d - 1, i] * scale[i][d]
        gathered[t_own, 2 * (base + SLOT[0]) + i] = acc

    own = gathered.at[t_own, pl.ds(2 * (base + SLOT[0]), 2)]
    gz = {}
    for d in FAR_FIRST:
        place = lax.rem(mz + d + NZ - 2, NZ) + SLOT[NZ - d]
        gz[d] = remote(
            own, gathered.at[t_own, pl.ds(2 * place, 2)], gz_s.at[d - 1], gz_r.at[d - 1], z_dev(d)
        )

    for r in range(B):
        acc = exps[r, 0] * lane_of(share, r)
        for t in range(1, T):
            acc = acc + exps[r, t] * lane_of(share, t * B + r)
        b = lax.rem(2 * base + r, B)
        imp_part[b // 4, pl.ds(lax.rem(b, 4), 1)] = jnp.sum(acc, axis=0, keepdims=True)
    y_copies = []
    for d in (2, 1, 3):
        y_copies.append(
            remote(
                imp_part.at[lax.rem(my + d, NY)], imp_in.at[d - 1], y_s.at[d - 1], y_r.at[d - 1],
                y_dev(d),
            )
        )

    spans = (NEAR, FAR)
    gx, gc = {}, []

    def span_of(t, g):
        first, count = spans[g]
        return gathered.at[t, pl.ds(2 * (base + first), 2 * count)]

    def forward_core(g, dx):
        span = span_of(t_half + lax.rem(mx + NX - dx, NX), g)
        gc.append(remote(span, span, gc_s.at[g, dx], gc_r.at[g, dx], core_dev()))

    for g, arrivals in enumerate(((1, 7, 2, 6), (3, 5, 4))):
        for d in arrivals:
            gz[d].wait_recv()
        span = span_of(t_own, g)
        for dx in (2, 1, 3):
            gx[g, dx] = remote(span, span, gx_s.at[g, dx - 1], gx_r.at[g, dx - 1], x_dev(dx))
        forward_core(g, 0)

    for copy in y_copies:
        copy.wait_recv()
    imp_ref[...] = imp_part[my] + imp_in[0] + imp_in[1] + imp_in[2]

    for g in range(2):
        for dx in (1, 3, 2):
            gx[g, dx].wait_recv()
            forward_core(g, dx)

    wrapped = lax.broadcasted_iota(jnp.int32, (B, D), 0) < shift

    def emit(half):
        for tl in range(NX):
            t = NX * half + tl
            for h in range(H):
                straight = gathered[t, 0:B, h, :]
                beyond = gathered[t, B : 2 * B, h, :]
                out_ref[t, :, h * D : (h + 1) * D] = jnp.where(wrapped, beyond, straight).astype(BF16)

    emit(mc)
    for copy in gc:
        copy.wait_recv()
    emit(other)

    for copy in started:
        copy.wait_send()


def on_device(queries, cache_keys, stored_values, new_keys, decoded_values, keep_mask):
    any_space = pl.BlockSpec(memory_space=pltpu.MemorySpace.HBM)
    vmem = pl.BlockSpec(memory_space=pltpu.VMEM)
    dma = pltpu.SemaphoreType.DMA
    return pl.pallas_call(
        kernel,
        out_shape=(
            jax.ShapeDtypeStruct((T, B, H * D), BF16),
            jax.ShapeDtypeStruct((B // NY, S), F32),
        ),
        in_specs=[any_space] * 6,
        out_specs=(vmem, vmem),
        scratch_shapes=[
            pltpu.VMEM((T, B, H, D), BF16),
            pltpu.VMEM((B, KV, S, D), BF16),
            pltpu.VMEM((B, KV, S, D), BF16),
            pltpu.VMEM((T, 2, KV, D), BF16),
            pltpu.VMEM((T, 2, KV, D), BF16),
            pltpu.VMEM((B, S), jnp.int32),
            pltpu.VMEM((B, T, H, D), F32),
            pltpu.VMEM((B, T, H, S), F32),
            pltpu.VMEM((H, D), F32),
            pltpu.VMEM((B, NX, H, D), F32),
            pltpu.VMEM((NX, B, H, D), F32),
            pltpu.VMEM((NX - 1, B, H, D), F32),
            pltpu.VMEM((NZ, 2, H, D), F32),
            pltpu.VMEM((NZ - 1, 2, H, D), F32),
            pltpu.VMEM((T, 2 * B, H, D), F32),
            pltpu.VMEM((NY, B // NY, S), F32),
            pltpu.VMEM((NY - 1, B // NY, S), F32),
            pltpu.VMEM((2, NX, B, H, D), F32),
            pltpu.VMEM((NX, B, H, D), F32),
            pltpu.VMEM((2, H, D), F32),
            pltpu.VMEM((2, H, D), F32),
            pltpu.VMEM((2, H, D), F32),
            pltpu.VMEM((NX - 1, 2, H, D), F32),
            pltpu.VMEM((2, H, D), F32),
            pltpu.VMEM((NZ - 1, 2, H, D), F32),
            dma((3,)),
            dma((3, NZ)),
            dma, dma, dma((2,)), dma((2,)),
            dma((NX - 1,)), dma((NX - 1,)), dma((2, NX - 1)), dma((2, NX - 1)),
            dma((NZ - 1,)), dma((NZ - 1,)), dma((NZ - 1,)), dma((NZ - 1,)),
            dma((NY - 1,)), dma((NY - 1,)),
            dma((NZ - 1,)), dma((NZ - 1,)), dma((2, NX - 1)), dma((2, NX - 1)),
            dma((2, NX)), dma((2, NX)),
        ],
        compiler_params=pltpu.CompilerParams(
            collective_id=0, has_side_effects=True, vmem_limit_bytes=63 << 20
        ),
    )(queries, cache_keys, stored_values, new_keys, decoded_values, keep_mask)


def solution(mesh):
    finer = Mesh(
        mesh.devices.reshape(mesh.shape["head"], NX, NZ, NC), ("head", "seq_0", "seq_1", "seq_2")
    )
    seq = ("seq_0", "seq_1", "seq_2")
    in_specs = (
        P(None, None, "head", None),
        P(None, "head", seq, None),
        P(None, "head", seq, None),
        P(None, None, "head", None),
        P(None, None, "head", None),
        P(None, seq),
    )
    out_specs = (P(None, None, "head"), P("head", seq))
    return jax.shard_map(
        on_device, mesh=finer, in_specs=in_specs, out_specs=out_specs, check_vma=False
    )
```

time: 40.5 us -> 35.5 us (0.88)
  Pallas kernels: 36.8 us -> 31.8 us
    pallas_call x1, Pallas kernels: 36.8 us -> 31.8 us  [on_device(): pl.pallas_call(kernel, out_shape=(jax.ShapeDtypeStruct((T, B, H * D), BF1...]
where the time goes in v2:
time: 35.5 us; the launch traced here: 35.4 us
  Pallas kernels  31.8 us (90%)
  local copies, waits for them, and re-layouts  2.92 us (8%)
  between operations  0.64 us (2%)
    pallas_call x1, Pallas kernels, on_device(): pl.pallas_call(kernel, out_shape=(jax.ShapeDtypeStruct((T, B, H * D), BF1...  31.8 us
    unnamed x2, local copies, waits for them, and re-layouts  2.92 us

profile of v2, /device:TPU:1, one launch (start us, length us, event | category | flops | bytes accessed | tf_op | source)
XLA Modules:
  0.0 35.4 jit_solution(4279559753612696786)
XLA Ops:
  0.6 31.8 %shard_map.77 = (bf16[8,16,1024]{2,1,0:T(8,128)(2,1)}, f32[4,128]{1,0:T(4,128)}) custom-call(bf16[8,16,8,128]{3,2,1,0:T(8,128)(2,1)} %q_hbm.1, bf16[16,4,128,128]{3,2,1,0:T(8,128)(2,1)} %k_hbm.1, bf16[16,4,128,128]{3,2,1,0:T(8,128)(2,1)} %v_hbm.1, bf16[8,16,4,128]{3,2,1,0:T(4,128)(2,1)} %nk_hbm.1, bf16[8,16,4,128]{3,2,1,0:T(4,128)(2,1)} %nv_hbm.1, ...), custom_call_target="tpu_custom_call" | custom-call | tf_op jit(solution)/shard_map/pallas_call | solution.py:398
  32.5 1.7 %copy.10 = bf16[8,16,1024]{2,1,0:T(8,128)(2,1)} copy(bf16[8,16,1024]{2,1,0:T(8,128)(2,1)} %get-tuple-element.4) | data formatting | bytes 524288
  34.1 1.2 %copy.11 = f32[4,128]{1,0:T(4,128)} copy(f32[4,128]{1,0:T(4,128)} %get-tuple-element.5) | data formatting | bytes 4096

commit v3 on v2

--- a/solution.py
+++ b/solution.py
@@ -391,16 +391,24 @@
         copy.wait_send()
 
 
+def store(attended, importance, attended_out, importance_out, sem):
+    copies = [
+        pltpu.make_async_copy(attended, attended_out, sem.at[0]),
+        pltpu.make_async_copy(importance, importance_out, sem.at[1]),
+    ]
+    for copy in copies:
+        copy.start()
+    for copy in copies:
+        copy.wait()
+
+
 def on_device(queries, cache_keys, stored_values, new_keys, decoded_values, keep_mask):
-    any_space = pl.BlockSpec(memory_space=pltpu.MemorySpace.HBM)
+    any_space = pl.BlockSpec(memory_space=pl.ANY)
     vmem = pl.BlockSpec(memory_space=pltpu.VMEM)
     dma = pltpu.SemaphoreType.DMA
-    return pl.pallas_call(
+    attended, importance = pl.pallas_call(
         kernel,
-        out_shape=(
-            jax.ShapeDtypeStruct((T, B, H * D), BF16),
-            jax.ShapeDtypeStruct((B // NY, S), F32),
-        ),
+        out_shape=(pltpu.VMEM((T, B, H * D), BF16), pltpu.VMEM((B // NY, S), F32)),
         in_specs=[any_space] * 6,
         out_specs=(vmem, vmem),
         scratch_shapes=[
@@ -442,6 +450,19 @@
             collective_id=0, has_side_effects=True, vmem_limit_bytes=63 << 20
         ),
     )(queries, cache_keys, stored_values, new_keys, decoded_values, keep_mask)
+    return pl.pallas_call(
+        store,
+        out_shape=(
+            jax.ShapeDtypeStruct((T, B, H * D), BF16),
+            jax.ShapeDtypeStruct((B // NY, S), F32),
+        ),
+        in_specs=[vmem, vmem],
+        out_specs=(any_space, any_space),
+        scratch_shapes=[dma((2,))],
+    )(
+        pltpu.with_memory_space_constraint(attended, pltpu.MemorySpace.VMEM),
+        pltpu.with_memory_space_constraint(importance, pltpu.MemorySpace.VMEM),
+    )
 
 
 def solution(mesh):

time: 35.5 us -> 32.6 us (0.918)
  local copies, waits for them, and re-layouts: 2.92 us -> 0 us
    unnamed x2 -> x0, local copies, waits for them, and re-layouts: 2.92 us -> none
    pallas_call x1 -> x2, Pallas kernels: 31.8 us -> 31.9 us  [the longest x1 31.1 us: on_device(): pl.pallas_call(kernel, out_shape=(pltpu.VMEM((T, B, H * D), BF16), pltpu....]
where the time goes in v3:
time: 32.6 us; the launch traced here: 32.5 us
  Pallas kernels  31.9 us (98%)
  between operations  0.64 us (2%)
    pallas_call x1, Pallas kernels, on_device(): pl.pallas_call(kernel, out_shape=(pltpu.VMEM((T, B, H * D), BF16), pltpu....  31.1 us
    pallas_call x1, Pallas kernels, on_device(): pl.pallas_call(store, out_shape=(jax.ShapeDtypeStruct((T, B, H * D), BF16...  0.72 us

profile of v3, /device:TPU:1, one launch (start us, length us, event | category | flops | bytes accessed | tf_op | source)
XLA Modules:
  0.0 32.5 jit_solution(12113878534214591254)
XLA Ops:
  0.6 31.1 %shard_map.77 = (bf16[8,16,1024]{2,1,0:T(8,128)(2,1)S(1)}, f32[4,128]{1,0:T(4,128)S(1)}) custom-call(bf16[8,16,8,128]{3,2,1,0:T(8,128)(2,1)} %q_hbm.1, bf16[16,4,128,128]{3,2,1,0:T(8,128)(2,1)} %k_hbm.1, bf16[16,4,128,128]{3,2,1,0:T(8,128)(2,1)} %v_hbm.1, bf16[8,16,4,128]{3,2,1,0:T(4,128)(2,1)} %nk_hbm.1, bf16[8,16,4,128]{3,2,1,0:T(4,128)(2,1)} %nv_hbm.1, ...), custom_call_target="tpu_custom_call" | custom-call | tf_op jit(solution)/shard_map/pallas_call | solution.py:409
  31.8 0.7 %shard_map.78 = (bf16[8,16,1024]{2,1,0:T(8,128)(2,1)}, f32[4,128]{1,0:T(4,128)}) custom-call(bf16[8,16,1024]{2,1,0:T(8,128)(2,1)S(1)} %get-tuple-element.4.attended, f32[4,128]{1,0:T(4,128)S(1)} %get-tuple-element.5.importance), custom_call_target="tpu_custom_call" | custom-call | tf_op jit(solution)/shard_map/pallas_call | solution.py:453

commit v4 on v3

--- a/solution.py
+++ b/solution.py
@@ -17,8 +17,13 @@
 S = 128
 NY, NX, NZ, NC = 4, 4, 8, 2
 FAR_FIRST = (4, 3, 5, 2, 6, 1, 7)
+OUT = FAR_FIRST + (0,)
 SLOT = [(d + 2) % NZ for d in range(NZ)]
+ROWS = [(2 * m + i, d, 2 * SLOT[d] + i) for m, d in enumerate(OUT) for i in range(2)]
+CORE_GROUPS = ((0, 3), (3, 5))
+X_GROUPS = ((0, 3), (3, 2), (5, 2), (7, 1))
 FAR, NEAR = (5, 3), (0, 5)
+BACK_GROUPS = ((2, 1, ()), (3, 2, (7, 6)), (0, 2, (1, 2)), (5, 3, (3, 5, 4)))
 HEADS_ALL = 32
 CONTEXT = S * NX * NZ * NC
 
@@ -47,7 +52,7 @@
     f_pair, f_x, stat_own, stat_core, stat_pair, stat_x, stat_group, stat_z,
     in_sem, chunk_sem,
     cs_s, cs_r, cd_s, cd_r, xs_s, xs_r, xd_s, xd_r, zs_s, zs_r, zd_s, zd_r, y_s, y_r,
-    gz_s, gz_r, gx_s, gx_r, gc_s, gc_r,
+    gz_s, gz_r, gx_s, gx_r, gc_s, gc_r, ready,
 ):
     my = lax.axis_index("head")
     mx = lax.axis_index("seq_0")
@@ -82,7 +87,7 @@
 
     barrier = pltpu.get_barrier_semaphore()
     partners = (
-        [z_dev(d) for d in FAR_FIRST]
+        [z_dev(d) for d in (2, 6, 1, 7)]
         + [x_dev(d) for d in (2, 1, 3)]
         + [y_dev(d) for d in (2, 1, 3)]
         + [core_dev()]
@@ -90,14 +95,17 @@
     for dev in partners:
         pl.semaphore_signal(barrier, inc=1, device_id=dev, device_id_type=MESH)
 
-    def chunk_loads(slot):
-        rows = pl.ds(2 * lax.rem(base + slot, NZ), 2)
-        mine = pl.ds(2 * slot, 2)
+    def chunk_loads(m):
+        rows = pl.ds(2 * lax.rem(mz + OUT[m], NZ), 2)
+        mine = pl.ds(2 * m, 2)
         return [
-            pltpu.make_async_copy(q_hbm.at[:, rows], q_ref.at[:, mine], chunk_sem.at[0, slot]),
-            pltpu.make_async_copy(k_hbm.at[rows], k_ref.at[mine], chunk_sem.at[1, slot]),
-            pltpu.make_async_copy(v_hbm.at[rows], v_ref.at[mine], chunk_sem.at[2, slot]),
+            pltpu.make_async_copy(q_hbm.at[:, rows], q_ref.at[:, mine], chunk_sem.at[0, m]),
+            pltpu.make_async_copy(k_hbm.at[rows], k_ref.at[mine], chunk_sem.at[1, m]),
+            pltpu.make_async_copy(v_hbm.at[rows], v_ref.at[mine], chunk_sem.at[2, m]),
         ]
+
+    def batch_row(d, i):
+        return 2 * lax.rem(mz + d, NZ) + i
 
     b_own = 2 * mz
     small = [
@@ -106,12 +114,10 @@
         pltpu.make_async_copy(nv_hbm.at[:, pl.ds(b_own, 2)], nv_ref, in_sem.at[2]),
     ]
     small[0].start()
-    loads = {slot: chunk_loads(slot) for slot in range(NZ)}
-    batches = ((4, 5, 6, 7), (0, 1, 2, 3))
-    for slots in batches:
-        for slot in slots:
-            for copy in loads[slot]:
-                copy.start()
+    loads = [chunk_loads(m) for m in range(NZ)]
+    for copies in loads:
+        for copy in copies:
+            copy.start()
     for copy in small[1:]:
         copy.start()
     small[0].wait()
@@ -121,13 +127,13 @@
 
     zero = jnp.zeros((H, D), F32)
     block_peak, block_total = zero, zero
-    for slots in batches:
-        for slot in slots:
-            for copy in loads[slot]:
+    for batch in (range(0, 4), range(4, 8)):
+        for m in batch:
+            for copy in loads[m]:
                 copy.wait()
-        rows = [2 * slot + i for slot in slots for i in range(2)]
+        rows = ROWS[2 * batch[0] : 2 * batch[-1] + 2]
         scores = []
-        for r in rows:
+        for r, _, _ in rows:
             q = q_ref[:, r].astype(F32).reshape(T * H, D).astype(BF16)
             wide = lax.dot_general(
                 q, k_ref[r].reshape(KV * S, D), (((1,), (1,)), ((), ())), preferred_element_type=F32
@@ -137,8 +143,8 @@
                 s = jnp.where(row_kv == k, wide[:, k * S : (k + 1) * S], s)
             scores.append(s * SCALE)
         weights = []
-        for r, s in zip(rows, scores):
-            b = lax.rem(2 * base + r, B)
+        for (r, d, at), s in zip(rows, scores):
+            b = batch_row(d, r % 2)
             keep = jnp.broadcast_to(mask_ref[pl.ds(b, 1), :], (T * H, S)) > 0
             m = jnp.max(jnp.where(keep, s, FAR_BELOW), axis=1, keepdims=True)
             e = jnp.where(keep, jnp.exp(s - m), 0.0)
@@ -146,11 +152,11 @@
             exps[r] = e.reshape(T, H, S)
             weights.append(e)
             for t in range(T):
-                here = lane == t * B + r
+                here = lane == t * B + at
                 part = slice(t * H, (t + 1) * H)
                 block_peak = jnp.where(here, jnp.broadcast_to(m[part], (H, D)), block_peak)
                 block_total = jnp.where(here, jnp.broadcast_to(total[part], (H, D)), block_total)
-        for r, e in zip(rows, weights):
+        for (r, _, _), e in zip(rows, weights):
             wide = jnp.concatenate(
                 [jnp.where(row_kv == k, e, 0.0).astype(BF16) for k in range(KV)], axis=1
             )
@@ -162,8 +168,8 @@
     for copy in small[1:]:
         copy.wait()
     for i in range(2):
-        r = 2 * SLOT[0] + i
-        here = lane == t_own * B + r
+        r = 2 * OUT.index(0) + i
+        here = lane == t_own * B + 2 * SLOT[0] + i
         q = q_ref[t_own, r].astype(F32)
         ns = []
         for j in range(T):
@@ -192,10 +198,12 @@
     stat_own[1] = total_tile
 
     pl.semaphore_wait(barrier, len(partners))
+    for d in (2, 6):
+        pl.semaphore_signal(ready, inc=1, device_id=z_dev(d), device_id_type=MESH)
 
     core_stat = remote(stat_own, stat_core, cs_s, cs_r, core_dev())
     core_copies = []
-    for g, (first, count) in enumerate((FAR, NEAR)):
+    for g, (first, count) in enumerate(CORE_GROUPS):
         rows = pl.ds(2 * first, 2 * count)
         core_copies.append(
             remote(
@@ -219,14 +227,15 @@
         )
     fo = to_front(f_own, t_half * B)
     fc = to_front(f_core, t_half * B)
-    for first, count in (FAR, NEAR):
+    for r, _, at in ROWS:
         for tl in range(NX):
-            for r in range(2 * first, 2 * (first + count)):
-                f_pair[0, tl, r] = lane_of(fo, tl * B + r)
-                f_pair[1, tl, r] = lane_of(fc, tl * B + r)
+            f_pair[0, tl, r] = lane_of(fo, tl * B + at)
+            f_pair[1, tl, r] = lane_of(fc, tl * B + at)
     x_copies = []
-    for g, (first, count) in enumerate((FAR, NEAR)):
-        core_copies[g].wait_recv()
+    for g, (first, count) in enumerate(X_GROUPS):
+        for h, (core_first, _) in enumerate(CORE_GROUPS):
+            if first == core_first:
+                core_copies[h].wait_recv()
         for tl in range(NX):
             for r in range(2 * first, 2 * (first + count)):
                 pair[tl, r] = (
@@ -273,30 +282,30 @@
     group_total = by_row(group_total)
     stat_group[0] = group_peak
     stat_group[1] = group_total
+    pl.semaphore_wait(ready, 2)
     z_stats = [
         remote(stat_group, stat_z.at[d - 1], zs_s.at[d - 1], zs_r.at[d - 1], z_dev(d))
         for d in FAR_FIRST
     ]
     for d in range(NX):
         f = to_front(factors[d], t_own * B)
-        for r in range(B):
-            f_x[d, r] = lane_of(f, r)
+        for r, _, at in ROWS:
+            f_x[d, r] = lane_of(f, at)
     z_copies = []
-    for g, sends in enumerate(((4, 3, 5), (2, 6, 1, 7, 0))):
+    for g, (first, count) in enumerate(X_GROUPS):
         for copy in x_copies[g]:
             copy.wait_recv()
-        for d in sends:
+        for m in range(first, first + count):
+            d = OUT[m]
             for i in range(2):
-                r = 2 * SLOT[d] + i
+                r = 2 * m + i
                 acc = pair[mx, r] * f_x[0, r]
                 for dx in range(1, NX):
                     acc = acc + x_in[dx - 1, r] * f_x[dx, r]
-                z_out[SLOT[d], i] = acc
+                z_out[m, i] = acc
             if d > 0:
                 z_copies.append(
-                    remote(
-                        z_out.at[SLOT[d]], z_in.at[d - 1], zd_s.at[d - 1], zd_r.at[d - 1], z_dev(d)
-                    )
+                    remote(z_out.at[m], z_in.at[d - 1], zd_s.at[d - 1], zd_r.at[d - 1], z_dev(d))
                 )
     for copy in z_stats:
         copy.wait_recv()
@@ -316,7 +325,7 @@
     for copy in z_copies:
         copy.wait_recv()
     for i in range(2):
-        acc = z_out[SLOT[0], i] * scale[i][0]
+        acc = z_out[OUT.index(0), i] * scale[i][0]
         for d in range(1, NZ):
             acc = acc + z_in[d - 1, i] * scale[i][d]
         gathered[t_own, 2 * (base + SLOT[0]) + i] = acc
@@ -329,11 +338,30 @@
             own, gathered.at[t_own, pl.ds(2 * place, 2)], gz_s.at[d - 1], gz_r.at[d - 1], z_dev(d)
         )
 
-    for r in range(B):
-        acc = exps[r, 0] * lane_of(share, r)
+    gx, gc = {}, []
+
+    def span_of(t, first, count):
+        return gathered.at[t, pl.ds(2 * (base + first), 2 * count)]
+
+    def forward_x(g):
+        first, count, arrivals = BACK_GROUPS[g]
+        for d in arrivals:
+            gz[d].wait_recv()
+        span = span_of(t_own, first, count)
+        for dx in (2, 1, 3):
+            gx[g, dx] = remote(span, span, gx_s.at[g, dx - 1], gx_r.at[g, dx - 1], x_dev(dx))
+
+    def forward_core(g, dx):
+        span = span_of(t_half + lax.rem(mx + NX - dx, NX), *(NEAR, FAR)[g])
+        gc.append(remote(span, span, gc_s.at[g, dx], gc_r.at[g, dx], core_dev()))
+
+    forward_x(0)
+
+    for r, d, at in ROWS:
+        acc = exps[r, 0] * lane_of(share, at)
         for t in range(1, T):
-            acc = acc + exps[r, t] * lane_of(share, t * B + r)
-        b = lax.rem(2 * base + r, B)
+            acc = acc + exps[r, t] * lane_of(share, t * B + at)
+        b = batch_row(d, r % 2)
         imp_part[b // 4, pl.ds(lax.rem(b, 4), 1)] = jnp.sum(acc, axis=0, keepdims=True)
     y_copies = []
     for d in (2, 1, 3):
@@ -344,33 +372,23 @@
             )
         )
 
-    spans = (NEAR, FAR)
-    gx, gc = {}, []
-
-    def span_of(t, g):
-        first, count = spans[g]
-        return gathered.at[t, pl.ds(2 * (base + first), 2 * count)]
-
-    def forward_core(g, dx):
-        span = span_of(t_half + lax.rem(mx + NX - dx, NX), g)
-        gc.append(remote(span, span, gc_s.at[g, dx], gc_r.at[g, dx], core_dev()))
-
-    for g, arrivals in enumerate(((1, 7, 2, 6), (3, 5, 4))):
-        for d in arrivals:
-            gz[d].wait_recv()
-        span = span_of(t_own, g)
-        for dx in (2, 1, 3):
-            gx[g, dx] = remote(span, span, gx_s.at[g, dx - 1], gx_r.at[g, dx - 1], x_dev(dx))
-        forward_core(g, 0)
+    forward_x(1)
+    forward_x(2)
+    forward_core(0, 0)
+    forward_x(3)
+    forward_core(1, 0)
 
     for copy in y_copies:
         copy.wait_recv()
     imp_ref[...] = imp_part[my] + imp_in[0] + imp_in[1] + imp_in[2]
 
-    for g in range(2):
-        for dx in (1, 3, 2):
+    for dx in (1, 3, 2):
+        for g in range(3):
             gx[g, dx].wait_recv()
-            forward_core(g, dx)
+        forward_core(0, dx)
+    for dx in (1, 3, 2):
+        gx[3, dx].wait_recv()
+        forward_core(1, dx)
 
     wrapped = lax.broadcasted_iota(jnp.int32, (B, D), 0) < shift
 
@@ -440,11 +458,12 @@
             dma((3,)),
             dma((3, NZ)),
             dma, dma, dma((2,)), dma((2,)),
-            dma((NX - 1,)), dma((NX - 1,)), dma((2, NX - 1)), dma((2, NX - 1)),
+            dma((NX - 1,)), dma((NX - 1,)), dma((4, NX - 1)), dma((4, NX - 1)),
             dma((NZ - 1,)), dma((NZ - 1,)), dma((NZ - 1,)), dma((NZ - 1,)),
             dma((NY - 1,)), dma((NY - 1,)),
-            dma((NZ - 1,)), dma((NZ - 1,)), dma((2, NX - 1)), dma((2, NX - 1)),
+            dma((NZ - 1,)), dma((NZ - 1,)), dma((4, NX - 1)), dma((4, NX - 1)),
             dma((2, NX)), dma((2, NX)),
+            pltpu.SemaphoreType.REGULAR,
         ],
         compiler_params=pltpu.CompilerParams(
             collective_id=0, has_side_effects=True, vmem_limit_bytes=63 << 20

time: 32.6 us -> 32.2 us (0.988)
  Pallas kernels: 31.9 us -> 31.5 us
    pallas_call x1, Pallas kernels: 31.1 us -> 30.7 us  [on_device(): pl.pallas_call(kernel, out_shape=(pltpu.VMEM((T, B, H * D), BF16), pltpu....]
where the time goes in v4:
time: 32.2 us; the launch traced here: 32.1 us
  Pallas kernels  31.5 us (98%)
  between operations  0.64 us (2%)
    pallas_call x1, Pallas kernels, on_device(): pl.pallas_call(kernel, out_shape=(pltpu.VMEM((T, B, H * D), BF16), pltpu....  30.7 us
    pallas_call x1, Pallas kernels, on_device(): pl.pallas_call(store, out_shape=(jax.ShapeDtypeStruct((T, B, H * D), BF16...  0.72 us

profile of v4, /device:TPU:1, one launch (start us, length us, event | category | flops | bytes accessed | tf_op | source)
XLA Modules:
  0.0 32.1 jit_solution(5373492635734012048)
XLA Ops:
  0.6 30.7 %shard_map.77 = (bf16[8,16,1024]{2,1,0:T(8,128)(2,1)S(1)}, f32[4,128]{1,0:T(4,128)S(1)}) custom-call(bf16[8,16,8,128]{3,2,1,0:T(8,128)(2,1)} %q_hbm.1, bf16[16,4,128,128]{3,2,1,0:T(8,128)(2,1)} %k_hbm.1, bf16[16,4,128,128]{3,2,1,0:T(8,128)(2,1)} %v_hbm.1, bf16[8,16,4,128]{3,2,1,0:T(4,128)(2,1)} %nk_hbm.1, bf16[8,16,4,128]{3,2,1,0:T(4,128)(2,1)} %nv_hbm.1, ...), custom_call_target="tpu_custom_call" | custom-call | tf_op jit(solution)/shard_map/pallas_call | solution.py:427
  31.4 0.7 %shard_map.78 = (bf16[8,16,1024]{2,1,0:T(8,128)(2,1)}, f32[4,128]{1,0:T(4,128)}) custom-call(bf16[8,16,1024]{2,1,0:T(8,128)(2,1)S(1)} %get-tuple-element.4.attended, f32[4,128]{1,0:T(4,128)S(1)} %get-tuple-element.5.importance), custom_call_target="tpu_custom_call" | custom-call | tf_op jit(solution)/shard_map/pallas_call | solution.py:472

commit v5 on v4

--- a/solution.py
+++ b/solution.py
@@ -20,8 +20,11 @@
 OUT = FAR_FIRST + (0,)
 SLOT = [(d + 2) % NZ for d in range(NZ)]
 ROWS = [(2 * m + i, d, 2 * SLOT[d] + i) for m, d in enumerate(OUT) for i in range(2)]
-CORE_GROUPS = ((0, 3), (3, 5))
-X_GROUPS = ((0, 3), (3, 2), (5, 2), (7, 1))
+FAR_ROWS = 2 * 3
+NEAR_GROUPS = ((3, 2), (5, 2), (7, 1))
+PEERS = [(dc, dx) for dc in range(NC) for dx in range(NX)]
+SIBLING = PEERS.index((1, 0))
+PEER_ORDER = (2, 6, 1, 3, 5, 7, 4)
 FAR, NEAR = (5, 3), (0, 5)
 BACK_GROUPS = ((2, 1, ()), (3, 2, (7, 6)), (0, 2, (1, 2)), (5, 3, (3, 5, 4)))
 HEADS_ALL = 32
@@ -48,11 +51,11 @@
     q_hbm, k_hbm, v_hbm, nk_hbm, nv_hbm, mask_hbm,
     out_ref, imp_ref,
     q_ref, k_ref, v_ref, nk_ref, nv_ref, mask_ref,
-    sums, exps, peaks, core_in, pair, x_in, z_out, z_in, gathered, imp_part, imp_in,
-    f_pair, f_x, stat_own, stat_core, stat_pair, stat_x, stat_group, stat_z,
+    sums, exps, peaks, core_in, far_in, pair, x_in, z_out, z_in, gathered, imp_part, imp_in,
+    f_pair, f_far, f_x, stat_own, stat_x, stat_group, stat_z,
     in_sem, chunk_sem,
-    cs_s, cs_r, cd_s, cd_r, xs_s, xs_r, xd_s, xd_r, zs_s, zs_r, zd_s, zd_r, y_s, y_r,
-    gz_s, gz_r, gx_s, gx_r, gc_s, gc_r, ready,
+    cd_s, cd_r, xs_s, xs_r, xf_s, xf_r, xd_s, xd_r, zs_s, zs_r, zd_s, zd_r, y_s, y_r,
+    gz_s, gz_r, gx_s, gx_r, ge_s, ge_r, gc_s, gc_r, ready,
 ):
     my = lax.axis_index("head")
     mx = lax.axis_index("seq_0")
@@ -66,6 +69,12 @@
     def core_dev():
         return {"seq_2": other}
 
+    def peer_core(p):
+        return other if PEERS[p][0] else mc
+
+    def peer_dev(p):
+        return {"seq_0": lax.rem(mx + PEERS[p][1], NX), "seq_2": peer_core(p)}
+
     def x_dev(d):
         return {"seq_0": lax.rem(mx + d, NX)}
 
@@ -85,10 +94,15 @@
         started.append(copy)
         return copy
 
+    def settle():
+        for copy in started:
+            copy.wait_send()
+        started.clear()
+
     barrier = pltpu.get_barrier_semaphore()
     partners = (
         [z_dev(d) for d in (2, 6, 1, 7)]
-        + [x_dev(d) for d in (2, 1, 3)]
+        + [peer_dev(p) for p in PEER_ORDER[:-1]]
         + [y_dev(d) for d in (2, 1, 3)]
         + [core_dev()]
     )
@@ -201,41 +215,36 @@
     for d in (2, 6):
         pl.semaphore_signal(ready, inc=1, device_id=z_dev(d), device_id_type=MESH)
 
-    core_stat = remote(stat_own, stat_core, cs_s, cs_r, core_dev())
-    core_copies = []
-    for g, (first, count) in enumerate(CORE_GROUPS):
-        rows = pl.ds(2 * first, 2 * count)
-        core_copies.append(
-            remote(
-                sums.at[rows, pl.ds(NX * other, NX)], core_in.at[rows], cd_s.at[g], cd_r.at[g],
-                core_dev(),
-            )
-        )
-    core_stat.wait_recv()
-    peak_c, total_c = stat_core[0], stat_core[1]
+    stats = [
+        remote(stat_own, stat_x.at[p - 1], xs_s.at[p - 1], xs_r.at[p - 1], peer_dev(p))
+        for p in PEER_ORDER
+    ]
+    far_rows = pl.ds(0, FAR_ROWS)
+    far_copies = [
+        remote(
+            sums.at[far_rows, NX * peer_core(p) + lax.rem(mx + PEERS[p][1], NX)],
+            far_in.at[p - 1], xf_s.at[p - 1], xf_r.at[p - 1], peer_dev(p),
+        )
+        for p in PEER_ORDER
+    ]
+
+    near_rows = pl.ds(FAR_ROWS, B - FAR_ROWS)
+    core_copy = remote(
+        sums.at[near_rows, pl.ds(NX * other, NX)], core_in.at[near_rows], cd_s, cd_r, core_dev()
+    )
+    stats[PEER_ORDER.index(SIBLING)].wait_recv()
+    peak_c = stat_x[SIBLING - 1, 0]
     pair_peak = jnp.maximum(peak_tile, peak_c)
-    f_own = jnp.exp(peak_tile - pair_peak)
-    f_core = jnp.exp(peak_c - pair_peak)
-    pair_total = total_tile * f_own + total_c * f_core
-    stat_pair[0] = pair_peak
-    stat_pair[1] = pair_total
-
-    x_stats = []
-    for d in (2, 1, 3):
-        x_stats.append(
-            remote(stat_pair, stat_x.at[d - 1], xs_s.at[d - 1], xs_r.at[d - 1], x_dev(d))
-        )
-    fo = to_front(f_own, t_half * B)
-    fc = to_front(f_core, t_half * B)
-    for r, _, at in ROWS:
+    fo = to_front(jnp.exp(peak_tile - pair_peak), t_half * B)
+    fc = to_front(jnp.exp(peak_c - pair_peak), t_half * B)
+    for r, _, at in ROWS[FAR_ROWS:]:
         for tl in range(NX):
             f_pair[0, tl, r] = lane_of(fo, tl * B + at)
             f_pair[1, tl, r] = lane_of(fc, tl * B + at)
+
+    core_copy.wait_recv()
     x_copies = []
-    for g, (first, count) in enumerate(X_GROUPS):
-        for h, (core_first, _) in enumerate(CORE_GROUPS):
-            if first == core_first:
-                core_copies[h].wait_recv()
+    for g, (first, count) in enumerate(NEAR_GROUPS):
         for tl in range(NX):
             for r in range(2 * first, 2 * (first + count)):
                 pair[tl, r] = (
@@ -251,17 +260,17 @@
                 for d in (2, 1, 3)
             ]
         )
-    for copy in x_stats:
-        copy.wait_recv()
-    group_peak = pair_peak
-    for d in range(1, NX):
-        group_peak = jnp.maximum(group_peak, stat_x[d - 1, 0])
-    factors = [jnp.exp(pair_peak - group_peak)]
-    group_total = pair_total * factors[0]
-    for d in range(1, NX):
-        f = jnp.exp(stat_x[d - 1, 0] - group_peak)
-        factors.append(f)
-        group_total = group_total + stat_x[d - 1, 1] * f
+    for p, copy in zip(PEER_ORDER, stats):
+        if p != SIBLING:
+            copy.wait_recv()
+    peer_peak = [peak_tile] + [stat_x[p - 1, 0] for p in range(1, len(PEERS))]
+    group_peak = peak_tile
+    for p in range(1, len(PEERS)):
+        group_peak = jnp.maximum(group_peak, peer_peak[p])
+    factors = [jnp.exp(one - group_peak) for one in peer_peak]
+    group_total = total_tile * factors[0]
+    for p in range(1, len(PEERS)):
+        group_total = group_total + stat_x[p - 1, 1] * factors[p]
 
     shift = 2 * base
     in_row = lax.rem(lane, B)
@@ -287,26 +296,44 @@
         remote(stat_group, stat_z.at[d - 1], zs_s.at[d - 1], zs_r.at[d - 1], z_dev(d))
         for d in FAR_FIRST
     ]
-    for d in range(NX):
-        f = to_front(factors[d], t_own * B)
-        for r, _, at in ROWS:
-            f_x[d, r] = lane_of(f, at)
+    for p in range(len(PEERS)):
+        f = to_front(factors[p], t_own * B)
+        for r, _, at in ROWS[:FAR_ROWS]:
+            f_far[p, r] = lane_of(f, at)
+    for dx in range(NX):
+        f = to_front(jnp.maximum(factors[dx], factors[NX + dx]), t_own * B)
+        for r, _, at in ROWS[FAR_ROWS:]:
+            f_x[dx, r] = lane_of(f, at)
     z_copies = []
-    for g, (first, count) in enumerate(X_GROUPS):
+
+    def send_z(m):
+        d = OUT[m]
+        if d > 0:
+            z_copies.append(
+                remote(z_out.at[m], z_in.at[d - 1], zd_s.at[d - 1], zd_r.at[d - 1], z_dev(d))
+            )
+
+    for copy in far_copies:
+        copy.wait_recv()
+    for m in range(FAR_ROWS // 2):
+        for i in range(2):
+            r = 2 * m + i
+            acc = sums[r, t_own] * f_far[0, r]
+            for p in range(1, len(PEERS)):
+                acc = acc + far_in[p - 1, r] * f_far[p, r]
+            z_out[m, i] = acc
+        send_z(m)
+    for g, (first, count) in enumerate(NEAR_GROUPS):
         for copy in x_copies[g]:
             copy.wait_recv()
         for m in range(first, first + count):
-            d = OUT[m]
             for i in range(2):
                 r = 2 * m + i
                 acc = pair[mx, r] * f_x[0, r]
                 for dx in range(1, NX):
                     acc = acc + x_in[dx - 1, r] * f_x[dx, r]
                 z_out[m, i] = acc
-            if d > 0:
-                z_copies.append(
-                    remote(z_out.at[m], z_in.at[d - 1], zd_s.at[d - 1], zd_r.at[d - 1], z_dev(d))
-                )
+            send_z(m)
     for copy in z_stats:
         copy.wait_recv()
     peak = group_peak
@@ -338,7 +365,7 @@
             own, gathered.at[t_own, pl.ds(2 * place, 2)], gz_s.at[d - 1], gz_r.at[d - 1], z_dev(d)
         )
 
-    gx, gc = {}, []
+    gx, ge, gc = {}, {}, []
 
     def span_of(t, first, count):
         return gathered.at[t, pl.ds(2 * (base + first), 2 * count)]
@@ -350,6 +377,10 @@
         span = span_of(t_own, first, count)
         for dx in (2, 1, 3):
             gx[g, dx] = remote(span, span, gx_s.at[g, dx - 1], gx_r.at[g, dx - 1], x_dev(dx))
+            if g == 3:
+                ge[dx] = remote(
+                    span, span, ge_s.at[dx - 1], ge_r.at[dx - 1], peer_dev(NX + dx)
+                )
 
     def forward_core(g, dx):
         span = span_of(t_half + lax.rem(mx + NX - dx, NX), *(NEAR, FAR)[g])
@@ -372,6 +403,8 @@
             )
         )
 
+    settle()
+
     forward_x(1)
     forward_x(2)
     forward_core(0, 0)
@@ -381,6 +414,8 @@
     for copy in y_copies:
         copy.wait_recv()
     imp_ref[...] = imp_part[my] + imp_in[0] + imp_in[1] + imp_in[2]
+
+    settle()
 
     for dx in (1, 3, 2):
         for g in range(3):
@@ -388,7 +423,6 @@
         forward_core(0, dx)
     for dx in (1, 3, 2):
         gx[3, dx].wait_recv()
-        forward_core(1, dx)
 
     wrapped = lax.broadcasted_iota(jnp.int32, (B, D), 0) < shift
 
@@ -401,12 +435,11 @@
                 out_ref[t, :, h * D : (h + 1) * D] = jnp.where(wrapped, beyond, straight).astype(BF16)
 
     emit(mc)
-    for copy in gc:
+    for copy in gc + list(ge.values()):
         copy.wait_recv()
     emit(other)
 
-    for copy in started:
-        copy.wait_send()
+    settle()
 
 
 def store(attended, importance, attended_out, importance_out, sem):
@@ -440,6 +473,7 @@
             pltpu.VMEM((B, T, H, S), F32),
             pltpu.VMEM((H, D), F32),
             pltpu.VMEM((B, NX, H, D), F32),
+            pltpu.VMEM((len(PEERS) - 1, FAR_ROWS, H, D), F32),
             pltpu.VMEM((NX, B, H, D), F32),
             pltpu.VMEM((NX - 1, B, H, D), F32),
             pltpu.VMEM((NZ, 2, H, D), F32),
@@ -448,21 +482,20 @@
             pltpu.VMEM((NY, B // NY, S), F32),
             pltpu.VMEM((NY - 1, B // NY, S), F32),
             pltpu.VMEM((2, NX, B, H, D), F32),
+            pltpu.VMEM((len(PEERS), FAR_ROWS, H, D), F32),
             pltpu.VMEM((NX, B, H, D), F32),
             pltpu.VMEM((2, H, D), F32),
-            pltpu.VMEM((2, H, D), F32),
-            pltpu.VMEM((2, H, D), F32),
-            pltpu.VMEM((NX - 1, 2, H, D), F32),
+            pltpu.VMEM((len(PEERS) - 1, 2, H, D), F32),
             pltpu.VMEM((2, H, D), F32),
             pltpu.VMEM((NZ - 1, 2, H, D), F32),
             dma((3,)),
             dma((3, NZ)),
-            dma, dma, dma((2,)), dma((2,)),
-            dma((NX - 1,)), dma((NX - 1,)), dma((4, NX - 1)), dma((4, NX - 1)),
+            dma, dma, dma((len(PEERS) - 1,)), dma((len(PEERS) - 1,)),
+            dma((len(PEERS) - 1,)), dma((len(PEERS) - 1,)), dma((3, NX - 1)), dma((3, NX - 1)),
             dma((NZ - 1,)), dma((NZ - 1,)), dma((NZ - 1,)), dma((NZ - 1,)),
             dma((NY - 1,)), dma((NY - 1,)),
             dma((NZ - 1,)), dma((NZ - 1,)), dma((4, NX - 1)), dma((4, NX - 1)),
-            dma((2, NX)), dma((2, NX)),
+            dma((NX - 1,)), dma((NX - 1,)), dma((2, NX)), dma((2, NX)),
             pltpu.SemaphoreType.REGULAR,
         ],
         compiler_params=pltpu.CompilerParams(

time: 32.2 us -> 32.1 us (level)
  no operation moved by 1% of the time
where the time goes in v5:
time: 32.1 us; the launch traced here: 32 us
  Pallas kernels  31.3 us (98%)
  between operations  0.64 us (2%)
    pallas_call x1, Pallas kernels, on_device(): pl.pallas_call(kernel, out_shape=(pltpu.VMEM((T, B, H * D), BF16), pltpu....  30.6 us
    pallas_call x1, Pallas kernels, on_device(): pl.pallas_call(store, out_shape=(jax.ShapeDtypeStruct((T, B, H * D), BF16...  0.72 us

profile of v5, /device:TPU:1, one launch (start us, length us, event | category | flops | bytes accessed | tf_op | source)
XLA Modules:
  0.0 32.0 jit_solution(13628883164543494271)
XLA Ops:
  0.6 30.6 %shard_map.77 = (bf16[8,16,1024]{2,1,0:T(8,128)(2,1)S(1)}, f32[4,128]{1,0:T(4,128)S(1)}) custom-call(bf16[8,16,8,128]{3,2,1,0:T(8,128)(2,1)} %q_hbm.1, bf16[16,4,128,128]{3,2,1,0:T(8,128)(2,1)} %k_hbm.1, bf16[16,4,128,128]{3,2,1,0:T(8,128)(2,1)} %v_hbm.1, bf16[8,16,4,128]{3,2,1,0:T(4,128)(2,1)} %nk_hbm.1, bf16[8,16,4,128]{3,2,1,0:T(4,128)(2,1)} %nv_hbm.1, ...), custom_call_target="tpu_custom_call" | custom-call | tf_op jit(solution)/shard_map/pallas_call | solution.py:460
  31.2 0.7 %shard_map.78 = (bf16[8,16,1024]{2,1,0:T(8,128)(2,1)}, f32[4,128]{1,0:T(4,128)}) custom-call(bf16[8,16,1024]{2,1,0:T(8,128)(2,1)S(1)} %get-tuple-element.4.attended, f32[4,128]{1,0:T(4,128)S(1)} %get-tuple-element.5.importance), custom_call_target="tpu_custom_call" | custom-call | tf_op jit(solution)/shard_map/pallas_call | solution.py:505

commit v6 on v5

--- a/solution.py
+++ b/solution.py
@@ -52,10 +52,10 @@
     out_ref, imp_ref,
     q_ref, k_ref, v_ref, nk_ref, nv_ref, mask_ref,
     sums, exps, peaks, core_in, far_in, pair, x_in, z_out, z_in, gathered, imp_part, imp_in,
-    f_pair, f_far, f_x, stat_own, stat_x, stat_group, stat_z,
+    f_pair, f_far, f_x, stat_own, stat_x, stat_group, stat_z, stat_full,
     in_sem, chunk_sem,
     cd_s, cd_r, xs_s, xs_r, xf_s, xf_r, xd_s, xd_r, zs_s, zs_r, zd_s, zd_r, y_s, y_r,
-    gz_s, gz_r, gx_s, gx_r, ge_s, ge_r, gc_s, gc_r, ready,
+    gz_s, gz_r, gx_s, gx_r, ge_s, ge_r, gc_s, gc_r, hs_s, hs_r, ready,
 ):
     my = lax.axis_index("head")
     mx = lax.axis_index("seq_0")
@@ -208,15 +208,21 @@
         sums[r, t_own] = sums[r, t_own] * f_old + new_sum * f_new
         peak_tile = jnp.where(here, both, peak_tile)
         total_tile = jnp.where(here, old_total * f_old + new_total * f_new, total_tile)
-    stat_own[0] = peak_tile
-    stat_own[1] = total_tile
+    low = lane < D // 2
+
+    def swap(tile):
+        return pltpu.roll(tile, D // 2, 1)
+
+    stat_own[0] = jnp.where(low, peak_tile, swap(total_tile))
+    stat_own[1] = jnp.where(low, swap(peak_tile), total_tile)
+    mine = stat_own[mc]
 
     pl.semaphore_wait(barrier, len(partners))
     for d in (2, 6):
         pl.semaphore_signal(ready, inc=1, device_id=z_dev(d), device_id_type=MESH)
 
     stats = [
-        remote(stat_own, stat_x.at[p - 1], xs_s.at[p - 1], xs_r.at[p - 1], peer_dev(p))
+        remote(stat_own.at[peer_core(p)], stat_x.at[p - 1], xs_s.at[p - 1], xs_r.at[p - 1], peer_dev(p))
         for p in PEER_ORDER
     ]
     far_rows = pl.ds(0, FAR_ROWS)
@@ -233,10 +239,10 @@
         sums.at[near_rows, pl.ds(NX * other, NX)], core_in.at[near_rows], cd_s, cd_r, core_dev()
     )
     stats[PEER_ORDER.index(SIBLING)].wait_recv()
-    peak_c = stat_x[SIBLING - 1, 0]
-    pair_peak = jnp.maximum(peak_tile, peak_c)
-    fo = to_front(jnp.exp(peak_tile - pair_peak), t_half * B)
-    fc = to_front(jnp.exp(peak_c - pair_peak), t_half * B)
+    peak_c = stat_x[SIBLING - 1]
+    pair_peak = jnp.maximum(mine, peak_c)
+    fo = jnp.exp(mine - pair_peak)
+    fc = jnp.exp(peak_c - pair_peak)
     for r, _, at in ROWS[FAR_ROWS:]:
         for tl in range(NX):
             f_pair[0, tl, r] = lane_of(fo, tl * B + at)
@@ -263,14 +269,14 @@
     for p, copy in zip(PEER_ORDER, stats):
         if p != SIBLING:
             copy.wait_recv()
-    peer_peak = [peak_tile] + [stat_x[p - 1, 0] for p in range(1, len(PEERS))]
-    group_peak = peak_tile
+    peer_peak = [mine] + [stat_x[p - 1] for p in range(1, len(PEERS))]
+    group_peak = mine
     for p in range(1, len(PEERS)):
         group_peak = jnp.maximum(group_peak, peer_peak[p])
     factors = [jnp.exp(one - group_peak) for one in peer_peak]
-    group_total = total_tile * factors[0]
+    group_total = swap(mine) * factors[0]
     for p in range(1, len(PEERS)):
-        group_total = group_total + stat_x[p - 1, 1] * factors[p]
+        group_total = group_total + swap(peer_peak[p]) * factors[p]
 
     shift = 2 * base
     in_row = lax.rem(lane, B)
@@ -289,19 +295,18 @@
 
     group_peak = by_row(group_peak)
     group_total = by_row(group_total)
-    stat_group[0] = group_peak
-    stat_group[1] = group_total
+    stat_group[...] = jnp.where(low, group_peak, swap(group_total))
     pl.semaphore_wait(ready, 2)
     z_stats = [
         remote(stat_group, stat_z.at[d - 1], zs_s.at[d - 1], zs_r.at[d - 1], z_dev(d))
         for d in FAR_FIRST
     ]
     for p in range(len(PEERS)):
-        f = to_front(factors[p], t_own * B)
+        f = to_front(factors[p], mx * B)
         for r, _, at in ROWS[:FAR_ROWS]:
             f_far[p, r] = lane_of(f, at)
     for dx in range(NX):
-        f = to_front(jnp.maximum(factors[dx], factors[NX + dx]), t_own * B)
+        f = to_front(jnp.maximum(factors[dx], factors[NX + dx]), mx * B)
         for r, _, at in ROWS[FAR_ROWS:]:
             f_x[dx, r] = lane_of(f, at)
     z_copies = []
@@ -338,17 +343,18 @@
         copy.wait_recv()
     peak = group_peak
     for d in range(1, NZ):
-        peak = jnp.maximum(peak, stat_z[d - 1, 0])
+        peak = jnp.maximum(peak, stat_z[d - 1])
     factors = [jnp.exp(group_peak - peak)]
     total = group_total * factors[0]
     for d in range(1, NZ):
-        f = jnp.exp(stat_z[d - 1, 0] - peak)
+        f = jnp.exp(stat_z[d - 1] - peak)
         factors.append(f)
-        total = total + stat_z[d - 1, 1] * f
+        total = total + swap(stat_z[d - 1]) * f
     inverse = 1.0 / total
-    front = [to_front(f * inverse, t_own * B + b_own) for f in factors]
+    front = [to_front(f * inverse, mx * B + b_own) for f in factors]
     scale = [[lane_of(f, i) for f in front] for i in range(2)]
-    share = jnp.exp(peaks[...] - by_slot(peak)) * by_slot(inverse) * (CONTEXT / (T * HEADS_ALL))
+    stat_full[mc] = jnp.where(low, peak, swap(total))
+    half_stat = remote(stat_full.at[mc], stat_full.at[mc], hs_s, hs_r, core_dev())
     for copy in z_copies:
         copy.wait_recv()
     for i in range(2):
@@ -388,6 +394,10 @@
 
     forward_x(0)
 
+    half_stat.wait_recv()
+    full_peak = by_slot(jnp.where(low, stat_full[0], swap(stat_full[1])))
+    full_total = by_slot(jnp.where(low, swap(stat_full[0]), stat_full[1]))
+    share = jnp.exp(peaks[...] - full_peak) / full_total * (CONTEXT / (T * HEADS_ALL))
     for r, d, at in ROWS:
         acc = exps[r, 0] * lane_of(share, at)
         for t in range(1, T):
@@ -485,9 +495,10 @@
             pltpu.VMEM((len(PEERS), FAR_ROWS, H, D), F32),
             pltpu.VMEM((NX, B, H, D), F32),
             pltpu.VMEM((2, H, D), F32),
-            pltpu.VMEM((len(PEERS) - 1, 2, H, D), F32),
+            pltpu.VMEM((len(PEERS) - 1, H, D), F32),
+            pltpu.VMEM((H, D), F32),
+            pltpu.VMEM((NZ - 1, H, D), F32),
             pltpu.VMEM((2, H, D), F32),
-            pltpu.VMEM((NZ - 1, 2, H, D), F32),
             dma((3,)),
             dma((3, NZ)),
             dma, dma, dma((len(PEERS) - 1,)), dma((len(PEERS) - 1,)),
@@ -496,6 +507,7 @@
             dma((NY - 1,)), dma((NY - 1,)),
             dma((NZ - 1,)), dma((NZ - 1,)), dma((4, NX - 1)), dma((4, NX - 1)),
             dma((NX - 1,)), dma((NX - 1,)), dma((2, NX)), dma((2, NX)),
+            dma, dma,
             pltpu.SemaphoreType.REGULAR,
         ],
         compiler_params=pltpu.CompilerParams(

time: 32.1 us -> 31.8 us (level)
  no operation moved by 1% of the time
where the time goes in v6:
time: 31.8 us; the launch traced here: 31.7 us
  Pallas kernels  31 us (97%)
  between operations  0.64 us (2%)
    pallas_call x1, Pallas kernels, on_device(): pl.pallas_call(kernel, out_shape=(pltpu.VMEM((T, B, H * D), BF16), pltpu....  30.3 us
    pallas_call x1, Pallas kernels, on_device(): pl.pallas_call(store, out_shape=(jax.ShapeDtypeStruct((T, B, H * D), BF16...  0.72 us

profile of v6, /device:TPU:1, one launch (start us, length us, event | category | flops | bytes accessed | tf_op | source)
XLA Modules:
  0.0 31.7 jit_solution(18032487122927320545)
XLA Ops:
  0.6 30.3 %shard_map.77 = (bf16[8,16,1024]{2,1,0:T(8,128)(2,1)S(1)}, f32[4,128]{1,0:T(4,128)S(1)}) custom-call(bf16[8,16,8,128]{3,2,1,0:T(8,128)(2,1)} %q_hbm.1, bf16[16,4,128,128]{3,2,1,0:T(8,128)(2,1)} %k_hbm.1, bf16[16,4,128,128]{3,2,1,0:T(8,128)(2,1)} %v_hbm.1, bf16[8,16,4,128]{3,2,1,0:T(4,128)(2,1)} %nk_hbm.1, bf16[8,16,4,128]{3,2,1,0:T(4,128)(2,1)} %nv_hbm.1, ...), custom_call_target="tpu_custom_call" | custom-call | tf_op jit(solution)/shard_map/pallas_call | solution.py:470
  30.9 0.7 %shard_map.78 = (bf16[8,16,1024]{2,1,0:T(8,128)(2,1)}, f32[4,128]{1,0:T(4,128)}) custom-call(bf16[8,16,1024]{2,1,0:T(8,128)(2,1)S(1)} %get-tuple-element.4.attended, f32[4,128]{1,0:T(4,128)S(1)} %get-tuple-element.5.importance), custom_call_target="tpu_custom_call" | custom-call | tf_op jit(solution)/shard_map/pallas_call | solution.py:517

commit v7 on v6

--- a/solution.py
+++ b/solution.py
@@ -454,9 +454,9 @@
 
 def store(attended, importance, attended_out, importance_out, sem):
     copies = [
-        pltpu.make_async_copy(attended, attended_out, sem.at[0]),
-        pltpu.make_async_copy(importance, importance_out, sem.at[1]),
-    ]
+        pltpu.make_async_copy(attended.at[pl.ds(2 * i, 2)], attended_out.at[pl.ds(2 * i, 2)], sem.at[i])
+        for i in range(T // 2)
+    ] + [pltpu.make_async_copy(importance, importance_out, sem.at[T // 2])]
     for copy in copies:
         copy.start()
     for copy in copies:
@@ -522,7 +522,7 @@
         ),
         in_specs=[vmem, vmem],
         out_specs=(any_space, any_space),
-        scratch_shapes=[dma((2,))],
+        scratch_shapes=[dma((T // 2 + 1,))],
     )(
         pltpu.with_memory_space_constraint(attended, pltpu.MemorySpace.VMEM),
         pltpu.with_memory_space_constraint(importance, pltpu.MemorySpace.VMEM),

time: 31.8 us -> 31.8 us (level)
  no operation moved by 1% of the time
where the time goes in v7:
time: 31.8 us; the launch traced here: 31.7 us
  Pallas kernels  31 us (97%)
  between operations  0.64 us (2%)
    pallas_call x1, Pallas kernels, on_device(): pl.pallas_call(kernel, out_shape=(pltpu.VMEM((T, B, H * D), BF16), pltpu....  30.3 us
    pallas_call x1, Pallas kernels, on_device(): pl.pallas_call(store, out_shape=(jax.ShapeDtypeStruct((T, B, H * D), BF16...  0.74 us

profile of v7, /device:TPU:1, one launch (start us, length us, event | category | flops | bytes accessed | tf_op | source)
XLA Modules:
  0.0 31.7 jit_solution(15189415525786881929)
XLA Ops:
  0.6 30.3 %shard_map.77 = (bf16[8,16,1024]{2,1,0:T(8,128)(2,1)S(1)}, f32[4,128]{1,0:T(4,128)S(1)}) custom-call(bf16[8,16,8,128]{3,2,1,0:T(8,128)(2,1)} %q_hbm.1, bf16[16,4,128,128]{3,2,1,0:T(8,128)(2,1)} %k_hbm.1, bf16[16,4,128,128]{3,2,1,0:T(8,128)(2,1)} %v_hbm.1, bf16[8,16,4,128]{3,2,1,0:T(4,128)(2,1)} %nk_hbm.1, bf16[8,16,4,128]{3,2,1,0:T(4,128)(2,1)} %nv_hbm.1, ...), custom_call_target="tpu_custom_call" | custom-call | tf_op jit(solution)/shard_map/pallas_call | solution.py:470
  30.9 0.7 %shard_map.78 = (bf16[8,16,1024]{2,1,0:T(8,128)(2,1)}, f32[4,128]{1,0:T(4,128)}) custom-call(bf16[8,16,1024]{2,1,0:T(8,128)(2,1)S(1)} %get-tuple-element.4.attended, f32[4,128]{1,0:T(4,128)S(1)} %get-tuple-element.5.importance), custom_call_target="tpu_custom_call" | custom-call | tf_op jit(solution)/shard_map/pallas_call | solution.py:517
